TPU v7x, 128 devices: a whole 4x4x4 slice. The times are simulated.
128 devices in a mesh: seq: 32 (over z, x, core), head: 4 (over y).
Axes of the slice: x: 4, y: 4, z: 4, core: 2. Of those that a mesh axis runs over, the one named last changes fastest.
Arguments:
- queries: bfloat16 [16384, 4096], P('seq', 'head'), may hold values from -24 to 24
- key_states: bfloat16 [16384, 4096], P('seq', 'head'), may hold values from -24 to 24
- value_states: bfloat16 [16384, 4096], P('seq', 'head'), may hold values from -6 to 6
- forward_out: bfloat16 [16384, 4096], P('seq', 'head'), may hold values from -3 to 3
- grad_out: bfloat16 [16384, 4096], P('seq', 'head'), may hold values from -96 to 96
- random_blocks: int32 [256, 32, 3], P(None, 'head'), may hold values from 0 to 255, as said below
- global_blocks: int32 [2], replicated, may hold values from 0 to 255, as said below
Outputs:
- grad_queries: bfloat16 [16384, 4096], P(('seq', 'head'))
- grad_keys: bfloat16 [16384, 4096], P(('seq', 'head'))
- grad_values: bfloat16 [16384, 4096], P(('seq', 'head'))
Inputs may be any that keep to these rules, and one draw needn't show every extreme that they name: `random_blocks`: for the query blocks of one shard of 512 tokens and the 8 heads of one head group, at most 8 of the 192 entries name blocks held by any one shard of 8 blocks, and one shard, the same for every group, is named exactly 8 times by every group. `global_blocks`: two different blocks, one of them the last block 255.
All inputs are finite; a program needn't handle non-finite values.
Results may differ from a plain program's by a relative error of at most 0.0053.
Values may be sent and summed in bfloat16 or wider, within the bound.
A program may use at most 128 MiB of HBM per device.

v0:
```python
from functools import partial

import jax
import jax.numpy as jnp
from jax import lax
from jax.sharding import PartitionSpec as P

DH = 128
BS = 64


def padded(cells, sides, width):
    for axis, dim in sides:
        count = lax.axis_size(axis)
        ends = count - 1
        head = lax.slice_in_dim(cells, 0, width, axis=dim)
        tail = lax.slice_in_dim(cells, cells.shape[dim] - width, cells.shape[dim], axis=dim)
        cells = jnp.concatenate(
            [
                lax.ppermute(tail, axis, [(i, (i + 1) % count) for i in range(ends)]),
                cells,
                lax.ppermute(head, axis, [((i + 1) % count, i) for i in range(ends)]),
            ],
            axis=dim,
        )
    return cells


def scaled(values):
    return values * DH ** (-0.5)


def attend(
    query_row_block,
    gradient_row_block,
    saved_rows,
    gathered_key_block,
    gathered_value_block,
    usable,
    outer_max,
    outer_sum,
):
    logit_scores = scaled(
        jnp.einsum(
            "zxp,zufp->zxuf",
            query_row_block,
            gathered_key_block,
            preferred_element_type=jnp.float32,
        )
    )
    logit_scores = jnp.where(usable[:, None, :, None], logit_scores, -jnp.inf)
    peak_score = jnp.maximum(jnp.max(logit_scores, axis=(2, 3)), outer_max)
    row_sum = jnp.sum(jnp.exp(logit_scores - peak_score[:, :, None, None]), axis=(2, 3))
    row_sum = row_sum + outer_sum * jnp.exp(outer_max - peak_score)
    log_norm = peak_score + jnp.log(row_sum)
    weights = jnp.exp(logit_scores - log_norm[:, :, None, None])
    row_dot = jnp.sum(
        gradient_row_block.astype(jnp.float32) * saved_rows.astype(jnp.float32), axis=-1
    )
    weight_gradient = jnp.einsum(
        "zxp,zufp->zxuf",
        gradient_row_block,
        gathered_value_block,
        preferred_element_type=jnp.float32,
    )
    dscores = weights * (weight_gradient - row_dot[:, :, None, None])
    weight_lowp = weights.astype(jnp.bfloat16)
    score_gradient_lowp = dscores.astype(jnp.bfloat16)
    dq_terms = scaled(
        jnp.einsum(
            "bqjk,bjkd->bqjd",
            score_gradient_lowp,
            gathered_key_block,
            preferred_element_type=jnp.float32,
        )
    )
    key_gradient_parts = scaled(
        jnp.einsum(
            "rmnf,rmc->rnfc",
            score_gradient_lowp,
            query_row_block,
            preferred_element_type=jnp.float32,
        )
    )
    value_gradient_parts = jnp.einsum(
        "rmnf,rmc->rnfc", weight_lowp, gradient_row_block, preferred_element_type=jnp.float32
    )
    return (log_norm, row_dot, dq_terms, key_gradient_parts, value_gradient_parts)


def head_pass(operands, usable):
    (
        query_row_block,
        gradient_row_block,
        saved_rows,
        wide_keys,
        wide_values,
        glob_keys,
        glob_values,
        far_keys,
        far_values,
        outer_max,
        outer_sum,
    ) = operands
    block_count = query_row_block.shape[0]

    def listed(wide_rows, glob_rows, far_rows):
        window_set = jnp.stack([wide_rows[:-2], wide_rows[1:-1], wide_rows[2:]], axis=1)
        glob_set = jnp.broadcast_to(glob_rows[None], (block_count,) + glob_rows.shape)
        return jnp.concatenate([window_set, glob_set, far_rows], axis=1)

    log_norm, row_dot, dq_terms, key_gradient_parts, value_gradient_parts = attend(
        query_row_block,
        gradient_row_block,
        saved_rows,
        listed(wide_keys, glob_keys, far_keys),
        listed(wide_values, glob_values, far_values),
        usable,
        outer_max,
        outer_sum,
    )
    far_query = lax.optimization_barrier(dq_terms[:, :, 5:].astype(jnp.bfloat16)).astype(
        jnp.float32
    )
    grad_query = jnp.sum(dq_terms[:, :, :5], axis=2) + jnp.sum(far_query, axis=2)

    def spread(slot_terms):
        widths = ((0, 0), (0, 0), (0, 0))
        first = jnp.pad(slot_terms[:, 0], ((0, 2),) + widths[1:])
        middle = jnp.pad(slot_terms[:, 1], ((1, 1),) + widths[1:])
        last_part = jnp.pad(slot_terms[:, 2], ((2, 0),) + widths[1:])
        return first + middle + last_part

    return (
        grad_query,
        log_norm,
        row_dot,
        spread(key_gradient_parts),
        spread(value_gradient_parts),
        jnp.sum(key_gradient_parts[:, 3:5], axis=0),
        jnp.sum(value_gradient_parts[:, 3:5], axis=0),
        key_gradient_parts[:, 5:].astype(jnp.bfloat16),
        value_gradient_parts[:, 5:].astype(jnp.bfloat16),
    )


def on_device(
    queries, key_states, value_states, forward_out, grad_out, random_blocks, global_blocks
):
    seq_count = lax.axis_size("seq")
    my_seq = lax.axis_index("seq")
    tokens = queries.shape[0]
    blocks = tokens // BS
    head_count = queries.shape[1] // DH
    requests = blocks * head_count * 3
    slot_count = max(2, (5 * requests + 4 * seq_count - 1) // (4 * seq_count))
    kv_pair = jnp.stack([key_states, value_states])
    kv_wide = padded(kv_pair, (("seq", 1),), BS)
    kv_heads = kv_wide.reshape(2, blocks + 2, BS, head_count, DH).transpose(0, 3, 1, 2, 4)
    kv_owned = kv_heads[:, :, 1:-1]
    kv_flat = (
        kv_pair.reshape(2, blocks, BS, head_count, DH)
        .transpose(0, 1, 3, 2, 4)
        .reshape(2, blocks * head_count, BS, DH)
    )
    glob_owner = global_blocks // blocks
    glob_local = global_blocks % blocks
    glob_mine = glob_owner == my_seq
    picked = kv_owned[:, :, glob_local] * glob_mine.astype(jnp.bfloat16)[None, None, :, None, None]
    glob_kv = lax.psum(picked, "seq").astype(jnp.float32).astype(jnp.bfloat16)
    table = random_blocks.reshape(seq_count, requests)
    owner_of = table // blocks
    local_of = table % blocks
    seq_ids = jnp.arange(seq_count, dtype=jnp.int32)
    onehot = (owner_of[:, :, None] == seq_ids[None, None, :]).astype(jnp.int32)
    before = jnp.cumsum(onehot, axis=1) - onehot
    rank_of = jnp.sum(before * onehot, axis=2)
    my_owner = lax.dynamic_index_in_dim(owner_of, my_seq, 0, keepdims=False)
    my_rank = lax.dynamic_index_in_dim(rank_of, my_seq, 0, keepdims=False)
    send_pos = my_owner * slot_count + my_rank
    request_ids = jnp.arange(requests, dtype=jnp.int32)
    pair_of = request_ids // 3
    spill_slot = seq_count * slot_count
    target = jnp.where(
        owner_of == my_seq, seq_ids[:, None] * slot_count + rank_of, spill_slot
    ).reshape(-1)
    head_all = jnp.broadcast_to(pair_of % head_count, (seq_count, requests)).reshape(-1)
    recv_block = (
        jnp.zeros((spill_slot + 1,), jnp.int32).at[target].set(local_of.reshape(-1))[:spill_slot]
    )
    recv_head = jnp.zeros((spill_slot + 1,), jnp.int32).at[target].set(head_all)[:spill_slot]
    recv_used = jnp.zeros((spill_slot + 1,), jnp.float32).at[target].set(1.0)[:spill_slot]
    recv_index = recv_block * head_count + recv_head

    def head_major(array):
        return array.reshape(blocks, BS, head_count, DH).transpose(2, 0, 1, 3)

    query_heads = head_major(queries)
    grad_heads = head_major(grad_out)
    saved_heads = head_major(forward_out)
    block_ids = jnp.arange(blocks)
    always = jnp.ones((blocks,), bool)
    has_prev = (block_ids > 0) | (my_seq > 0)
    has_next = (block_ids < blocks - 1) | (my_seq < seq_count - 1)
    outgoing = kv_flat[:, recv_index]
    incoming = lax.all_to_all(outgoing, "seq", split_axis=1, concat_axis=1, tiled=True)
    fetched = (
        incoming[:, send_pos].reshape(2, blocks, head_count, 3, BS, DH).transpose(0, 2, 1, 3, 4, 5)
    )
    usable = jnp.stack([has_prev, always, has_next, always, always, always, always, always], axis=1)
    outer_max = jnp.full((head_count, blocks, BS), -jnp.inf, jnp.float32)
    outer_sum = jnp.zeros((head_count, blocks, BS), jnp.float32)
    results = lax.map(
        partial(head_pass, usable=usable),
        (
            query_heads,
            grad_heads,
            saved_heads,
            kv_heads[0],
            kv_heads[1],
            glob_kv[0],
            glob_kv[1],
            fetched[0],
            fetched[1],
            outer_max,
            outer_sum,
        ),
    )
    grad_query = results[0]
    far_pack = (
        jnp.stack([results[7], results[8]]).transpose(0, 2, 1, 3, 4, 5).reshape(2, requests, BS, DH)
    )
    sendback = jnp.zeros((2, spill_slot, BS, DH), jnp.bfloat16).at[:, send_pos].set(far_pack)
    returned = lax.all_to_all(sendback, "seq", split_axis=1, concat_axis=1, tiled=True)
    far_grads = returned.astype(jnp.float32) * recv_used[None, :, None, None]
    owned_far = (
        jnp.zeros((2, blocks * head_count, BS, DH), jnp.float32).at[:, recv_index].add(far_grads)
    )
    rim_pack = jnp.stack([results[3], results[4]])
    rim_out = jnp.concatenate([rim_pack[:, :, 0], rim_pack[:, :, -1]], axis=2)
    rim_in = padded(rim_out, (("seq", 2),), BS)
    owned = rim_pack[:, :, 1:-1]
    owned = owned.at[:, :, 0].add(rim_in[:, :, :BS]).at[:, :, -1].add(rim_in[:, :, -BS:])
    glob_sum = lax.psum(jnp.stack([results[5], results[6]]), "seq")
    glob_sum = glob_sum * glob_mine.astype(jnp.float32)[None, None, :, None, None]
    owned = owned.at[:, :, glob_local].add(glob_sum)
    owned = owned + owned_far.reshape(2, blocks, head_count, BS, DH).transpose(0, 2, 1, 3, 4)
    grads_kv = (
        owned.astype(jnp.bfloat16).transpose(0, 2, 3, 1, 4).reshape(2, tokens, head_count * DH)
    )
    dq_rows = grad_query.astype(jnp.bfloat16).transpose(1, 2, 0, 3).reshape(tokens, head_count * DH)
    out_query, out_keys, out_values = (
        lax.all_to_all(dq_rows, "head", split_axis=0, concat_axis=1, tiled=True),
        lax.all_to_all(grads_kv[0], "head", split_axis=0, concat_axis=1, tiled=True),
        lax.all_to_all(grads_kv[1], "head", split_axis=0, concat_axis=1, tiled=True),
    )
    return (out_query, out_keys, out_values)


def solution(mesh):
    return jax.shard_map(
        on_device,
        mesh=mesh,
        in_specs=(
            P("seq", "head"),
            P("seq", "head"),
            P("seq", "head"),
            P("seq", "head"),
            P("seq", "head"),
            P(None, "head", None),
            P(),
        ),
        out_specs=(P(("seq", "head"), None), P(("seq", "head"), None), P(("seq", "head"), None)),
        check_vma=False,
    )
```

profile of v0, /device:TPU:33, one launch (start us, length us, event | category | flops | bytes accessed | tf_op | source)
XLA Modules:
  0.0 853.3 jit_solution(16249413253305519232)
XLA Ops:
  10.5 18.4 %reduce-window.6 = s32[32,32,2,128]{3,1,2,0:T(8,128)S(1)} reduce-window(s32[32,32,2,128]{3,1,2,0:T(8,128)S(1)} %copy_bitcast_fusion.1, s32[]{:T(128)} %constant.212.clone.1), window={size=1x1x1x128 pad=0_0x0_0x0_0x127_0}, to_apply=%region_1.2 | reduce-window | flops 33292288 | bytes 2097156 | tf_op jit(solution)/shard_map/reduce-window
  31.0 23.0 %scatter_custom_fusion = s32[257]{0:T(512)S(1)} fusion(s32[6144]{0:T(1024)S(1)} %bitcast.346, s32[6144]{0:T(1024)S(1)} %add_select_fusion.1, s32[]{:T(128)} %constant.212.clone.1), kind=kCustom, calls=%fused_computation.170 | custom fusion | bytes 1032 | tf_op jit(solution)/shard_map/scatter | solution.py:189
  54.0 23.0 %scatter_custom_fusion.1 = s32[257]{0:T(512)S(1)} fusion(s32[6144]{0:T(1024)S(1)} %bitcast.347, s32[6144]{0:T(1024)S(1)} %reshape.454, s32[]{:T(128)} %constant.212.clone.1), kind=kCustom, calls=%fused_computation.168 | custom fusion | bytes 1032 | tf_op jit(solution)/shard_map/scatter | solution.py:191
  78.3 8.6 %gather_fusion.1 = bf16[256,2,64,128]{3,2,1,0:T(8,128)(2,1)} fusion(bf16[2,64,64,128]{3,2,1,0:T(8,128)(2,1)S(1)} %bitcast.306, s32[1024]{0:T(1024)S(1)} %pad_clamp_fusion.1), kind=kCustom, calls=%fused_computation.1 | custom fusion | bytes 16778240 | tf_op jit(solution)/shard_map/gather | solution.py:205
  87.0 8.5 all-to-all-start
  96.4 3.4 collective-permute-start
  99.8 1.9 collective-permute-start.1
  103.0 2.5 copy.179
  106.8 1.4 bitcast_bitcast_fusion.2
  108.2 2.3 bitcast_bitcast_fusion.1
  112.8 2.5 copy.130
  116.7 77.6 %collective-permute-done = bf16[2,64,1024]{2,1,0:T(8,128)(2,1)S(1)} collective-permute-done((bf16[2,64,1024]{2,1,0:T(8,128)(2,1)}, bf16[2,64,1024]{2,1,0:T(8,128)(2,1)S(1)}, u32[]{:S(2)}, u32[]{:S(2)}) %collective-permute-start) | collective-permute-done | bytes 262176 | tf_op jit(solution)/shard_map/ppermute | solution.py:20
  194.8 1.4 pad_maximum_fusion.1
  197.6 1.6 slice.285
  199.1 2.2 gather_fusion
  202.3 2.4 slice_bitcast_fusion.8
  204.7 108.3 %all-reduce.10.cloned.1.call-done = bf16[2,8,2,64,128]{4,3,1,0,2:T(8,128)(2,1)} async-done(((bf16[2,8,2,64,128]{4,3,1,0,2:T(8,128)(2,1)}), bf16[2,8,2,64,128]{4,3,1,0,2:T(8,128)(2,1)}) %all-reduce.10.cloned.1.call-update) | async-done | bytes 524304 | tf_op jit(solution)/shard_map/psum | solution.py:170
  314.1 11.5 %gather_fusion.2 = bf16[192,2,64,128]{3,2,1,0:T(8,128)(2,1)} fusion(bf16[2,256,64,128]{3,2,0,1:T(8,128)(2,1)} %all-to-all-done, s32[1024]{0:T(1024)S(1)} %pad_clamp_fusion), kind=kCustom, calls=%fused_computation.2 | custom fusion | bytes 12583680 | tf_op jit(solution)/shard_map/gather | solution.py:208
  325.5 4.3 copy.126
  329.8 4.1 slice_bitcast_fusion.6
  334.0 149.5 %while.26 = (s32[]{:T(128)}, bf16[8,8,64,128]{3,2,1,0:T(8,128)(2,1)S(1)}, f32[8,10,64,128]{3,2,0,1:T(8,128)}, f32[8,10,64,128]{3,2,0,1:T(8,128)}, f32[8,2,64,128...) while((s32[]{:T(128)}, ...), condition=%wide.region_14.15_spmd, body=%wide.region_6.14_spmd.sunk | while | flops 340951552 | bytes 32071516 | solution.py:213
  337.9 1.4 fusion.90
  346.1 1.4 multiply_convert_fusion.2
  364.7 1.4 multiply_convert_fusion.2
  375.2 1.4 fusion.90
  383.3 1.4 multiply_convert_fusion.2
  402.0 1.4 multiply_convert_fusion.2
  412.5 1.4 fusion.90
  420.7 1.4 multiply_convert_fusion.2
  431.3 1.4 fusion.90
  439.5 1.4 multiply_convert_fusion.2
  458.1 1.4 multiply_convert_fusion.2
  468.6 1.4 fusion.90
  476.7 1.5 multiply_convert_fusion.2
  483.5 3.8 pad_maximum_fusion
  487.3 4.1 copy.142
  491.3 5.5 broadcast_in_dim.140
  496.8 29.1 %scatter_fusion = bf16[2,256,64,128]{3,2,1,0:T(8,128)(2,1)} fusion(bf16[2,256,64,128]{3,2,1,0:T(8,128)(2,1)} %broadcast_in_dim.140, s32[192]{0:T(256)S(1)} %bitcast.350, bf16[192,2,64,128]{3,2,1,0:T(8,128)(2,1)} %copy.142), kind=kCustom, calls=%fused_computation.5 | custom fusion | bytes 18875136 | tf_op jit(solution)/shard_map/scatter | solution.py:233
  525.9 9.7 %copy.143 = bf16[2,256,64,128]{3,2,0,1:T(8,128)(2,1)} copy(bf16[2,256,64,128]{3,2,1,0:T(8,128)(2,1)} %scatter_fusion) | data formatting | bytes 16777216 | tf_op jit(solution)/shard_map/scatter | solution.py:233
  535.6 6.9 all-to-all-start.2
  542.6 1.8 fusion.31
  544.4 3.4 collective-permute-start.2
  548.9 2.2 fusion.27
  551.1 95.6 %collective-permute-done.2 = f32[2,8,64,128]{3,2,1,0:T(8,128)} collective-permute-done((f32[2,8,64,128]{3,2,1,0:T(8,128)}, f32[2,8,64,128]{3,2,1,0:T(8,128)}, u32[]{:S(2)}, u32[]{:S(2)}) %collective-permute-start.2) | collective-permute-done | bytes 524320 | tf_op jit(solution)/shard_map/ppermute | solution.py:20
  647.9 2.0 copy-done.2
  649.9 2.0 collective-permute-start.3
  652.0 23.0 %scatter_custom_fusion.3 = f32[257]{0:T(512)S(1)} fusion(s32[6144]{0:T(1024)S(1)} %bitcast.348, f32[6144]{0:T(1024)S(1)} %broadcast.368, f32[]{:T(128)} %constant.213.clone.1), kind=kCustom, calls=%fused_computation.166 | custom fusion | bytes 1032 | tf_op jit(solution)/shard_map/scatter | solution.py:192
  674.9 1.9 copy.134
  678.1 39.9 %all-reduce.12.cloned.1.call-done = f32[2,8,2,64,128]{4,3,2,1,0:T(8,128)} async-done(((f32[2,8,2,64,128]{4,3,2,1,0:T(8,128)}), f32[2,8,2,64,128]{4,3,2,1,0:T(8,128)}) %all-reduce.12.cloned.1.call-update) | async-done | bytes 1048592 | tf_op jit(solution)/shard_map/psum | solution.py:244
  718.0 1.6 multiply_bitcast_fusion.2
  720.6 2.2 copy.139
  723.7 4.3 all-to-all-start.1
  728.0 10.4 %multiply_bitcast_fusion.1 = f32[256,2,64,128]{3,2,1,0:T(8,128)} fusion(bf16[2,256,64,128]{3,2,0,1:T(8,128)(2,1)} %all-to-all-done.2, f32[256]{0:T(256)S(1)} %slice-done), kind=kLoop, calls=%fused_computation.73 | loop fusion | flops 8388608 | bytes 25166848 | tf_op jit(solution)/shard_map/mul | solution.py:235
  738.3 2.5 broadcast_in_dim.139
  740.8 51.8 %scatter_fusion.1 = f32[2,64,64,128]{3,2,1,0:T(8,128)} fusion(f32[2,64,64,128]{3,2,1,0:T(8,128)} %broadcast_in_dim.139, s32[256]{0:T(256)S(1)} %compare_select_fusion.6, f32[256,2,64,128]{3,2,1,0:T(8,128)} %multiply_bitcast_fusion.1), kind=kCustom, calls=%fused_computation.7 | custom fusion | flops 4194304 | bytes 50332672 | tf_op jit(solution)/shard_map/scatter-add | solution.py:237
  792.6 6.8 bitcast_add_fusion
  799.4 3.1 scatter_fusion.2
  802.5 2.7 convert_bitcast_fusion
  808.3 4.4 all-to-all-start.3
  812.7 1.9 copy.148
  815.9 11.2 %all-to-all-done.3 = bf16[4,128,1024]{2,1,0:T(8,128)(2,1)S(1)} async-done(((bf16[4,128,1024]{2,1,0:T(8,128)(2,1)}), bf16[4,128,1024]{2,1,0:T(8,128)(2,1)S(1)}, u32[]{:S(2)}, u32[]{:S(2)}) %all-to-all-start.3) | async-done | bytes 1048608 | tf_op jit(solution)/shard_map/all_to_all | solution.py:254
  827.1 3.5 all-to-all-start.4
  831.9 2.3 copy.150
  836.1 7.9 all-to-all-done.4
  (349 shorter events, 162.1 us)
Async XLA Ops:
  29.0 48.0 %copy-start.5 = (bf16[512,1024]{1,0:T(8,128)(2,1)S(1)}, bf16[512,1024]{1,0:T(8,128)(2,1)}, u32[]{:S(2)}) copy-start(bf16[512,1024]{1,0:T(8,128)(2,1)} %param.14) | copy-start | bytes 3145732
  29.8 47.5 %copy-start.4 = (bf16[512,1024]{1,0:T(8,128)(2,1)S(1)}, bf16[512,1024]{1,0:T(8,128)(2,1)}, u32[]{:S(2)}) copy-start(bf16[512,1024]{1,0:T(8,128)(2,1)} %param.15) | copy-start | bytes 3145732
  87.0 8.6 %copy-start.6 = (bf16[512,1024]{1,0:T(8,128)(2,1)S(1)}, bf16[512,1024]{1,0:T(8,128)(2,1)}, u32[]{:S(2)}) copy-start(bf16[512,1024]{1,0:T(8,128)(2,1)} %param.14) | copy-start | bytes 3145732
  87.0 227.1 %all-to-all-start = ((bf16[2,256,64,128]{3,2,0,1:T(8,128)(2,1)}), bf16[2,256,64,128]{3,2,0,1:T(8,128)(2,1)}, u32[]{:S(2)}, u32[]{:S(2)}) async-start(bf16[2,256,64,128]{3,2,0,1:T(8,128)(2,1)} %bitcast.307), calls=%async_computation | async-start | bytes 16777216 | tf_op jit(solution)/shard_map/all_to_all | solution.py:206
  95.5 6.2 copy-start.9
  95.5 217.5 %all-reduce.10.cloned.1.call-start = ((), (), s32[]{:S(2)}) async-start(), calls=%async_computation.5 | async-start | bytes 1048576 | tf_op jit(solution)/shard_map/psum | solution.py:170
  96.4 97.9 %collective-permute-start = (bf16[2,64,1024]{2,1,0:T(8,128)(2,1)}, bf16[2,64,1024]{2,1,0:T(8,128)(2,1)S(1)}, u32[]{:S(2)}, u32[]{:S(2)}) collective-permute-start(bf16[2,64,1024]{2,1,0:T(8,128)(2,1)} %get-tuple-element.381), channel_id=1, source_target_pairs={{0,4},{4,8},{8,12},{12,16},{16,20},{20,24},{24,28},{28,32},{32,36}... | collective-permute-start | bytes 786440 | tf_op jit(solution)/shard_map/ppermute | solution.py:20
  99.8 95.1 %collective-permute-start.1 = (bf16[2,64,1024]{2,1,0:T(8,128)(2,1)}, bf16[2,64,1024]{2,1,0:T(8,128)(2,1)}, u32[]{:S(2)}, u32[]{:S(2)}) collective-permute-start(bf16[2,64,1024]{2,1,0:T(8,128)(2,1)} %get-tuple-element.382), channel_id=1, source_target_pairs={{4,0},{8,4},{12,8},{16,12},{20,16},{24,20},{28,24},{32,28},{36,32}... | collective-permute-start | bytes 786440 | tf_op jit(solution)/shard_map/ppermute | solution.py:22
  101.7 3.8 copy-start.10
  101.7 5.0 copy-start.16
  106.7 3.7 copy-start.8
  111.6 3.8 copy-start.7
  329.8 4.2 copy-start.11
  329.8 4.2 copy-start.13
  483.4 3.8 copy-start.12
  535.6 7.0 copy-start
  535.6 188.1 %all-to-all-start.2 = ((bf16[2,256,64,128]{3,2,0,1:T(8,128)(2,1)}), bf16[2,256,64,128]{3,2,0,1:T(8,128)(2,1)}, u32[]{:S(2)}, u32[]{:S(2)}) async-start(bf16[2,256,64,128]{3,2,0,1:T(8,128)(2,1)} %copy.143), calls=%async_computation.2 | async-start | bytes 16777216 | tf_op jit(solution)/shard_map/all_to_all | solution.py:234
  542.5 175.5 %all-reduce.12.cloned.1.call-start = ((), (), s32[]{:S(2)}) async-start(), calls=%async_computation.6 | async-start | bytes 2097152 | tf_op jit(solution)/shard_map/psum | solution.py:244
  542.6 5.2 copy-start.14
  544.4 102.3 %collective-permute-start.2 = (f32[2,8,64,128]{3,2,1,0:T(8,128)}, f32[2,8,64,128]{3,2,1,0:T(8,128)}, u32[]{:S(2)}, u32[]{:S(2)}) collective-permute-start(f32[2,8,64,128]{3,2,1,0:T(8,128)} %fusion.31), channel_id=1, source_target_pairs={{0,4},{4,8},{8,12},{12,16},{16,20},{20,24},{24,28},{28,32},{32,36}... | collective-permute-start | bytes 1572872 | tf_op jit(solution)/shard_map/ppermute | solution.py:20
  548.9 97.8 %copy-start.1 = (f32[8,10,64,128]{3,2,0,1:T(8,128)S(1)}, f32[8,10,64,128]{3,2,0,1:T(8,128)}, u32[]{:S(2)}) copy-start(f32[8,10,64,128]{3,2,0,1:T(8,128)} %get-tuple-element.255) | copy-start | bytes 7864324
  647.9 2.0 copy-start.2
  649.9 72.9 %collective-permute-start.3 = (f32[2,8,64,128]{3,2,1,0:T(8,128)S(1)}, f32[2,8,64,128]{3,2,1,0:T(8,128)S(1)}, u32[]{:S(2)}, u32[]{:S(2)}) collective-permute-start(f32[2,8,64,128]{3,2,1,0:T(8,128)S(1)} %get-tuple-element.375), channel_id=1, source_target_pairs={{4,0},{8,4},{12,8},{16,12},{20,16},{24,20},{28,24},{32,28},{36,32}... | collective-permute-start | bytes 1572872 | tf_op jit(solution)/shard_map/ppermute | solution.py:22
  674.9 44.7 %copy-start.15 = (f32[257]{0:T(512)}, f32[257]{0:T(512)S(1)}, u32[]{:S(2)}) copy-start(f32[257]{0:T(512)S(1)} %scatter_custom_fusion.3) | copy-start | bytes 3088
  718.0 2.5 copy-start.3
  722.8 5.1 slice-start
  723.7 84.7 %all-to-all-start.1 = ((bf16[4,128,1024]{2,1,0:T(8,128)(2,1)}), bf16[4,128,1024]{2,1,0:T(8,128)(2,1)S(1)}, u32[]{:S(2)}, u32[]{:S(2)}) async-start(bf16[4,128,1024]{2,1,0:T(8,128)(2,1)} %all_to_all.49), calls=%async_computation.1 | async-start | bytes 2097152 | tf_op jit(solution)/shard_map/all_to_all | solution.py:253
  808.3 18.7 %all-to-all-start.3 = ((bf16[4,128,1024]{2,1,0:T(8,128)(2,1)}), bf16[4,128,1024]{2,1,0:T(8,128)(2,1)S(1)}, u32[]{:S(2)}, u32[]{:S(2)}) async-start(bf16[4,128,1024]{2,1,0:T(8,128)(2,1)} %all_to_all.54), calls=%async_computation.3 | async-start | bytes 2097152 | tf_op jit(solution)/shard_map/all_to_all | solution.py:254
  827.1 17.0 %all-to-all-start.4 = ((bf16[4,128,1024]{2,1,0:T(8,128)(2,1)}), bf16[4,128,1024]{2,1,0:T(8,128)(2,1)S(1)}, u32[]{:S(2)}, u32[]{:S(2)}) async-start(bf16[4,128,1024]{2,1,0:T(8,128)(2,1)} %all_to_all.58), calls=%async_computation.4 | async-start | bytes 2097152 | tf_op jit(solution)/shard_map/all_to_all | solution.py:255
Sparse Core Ops, SparseCore 0:
  202.4 110.4 all-reduce.9
  549.0 168.9 all-reduce.11
where the time goes:
time: 869 us; the launch traced here: 853 us
  waiting for transfers between devices  341 us (39%)
  local copies, waits for them, and re-layouts  277 us (32%)
  other arithmetic  132 us (15%)
  matrix products  47.9 us (6%)
  starting transfers between devices  38.3 us (4%)
  between operations  15.1 us (2%)
    ppermute x2, waiting for transfers between devices, padded(): lax.ppermute(tail, axis, [(i, (i + 1) % count) for i in range(ends)])  173 us
    psum x1, waiting for transfers between devices, on_device(): glob_kv = lax.psum(picked, 'seq').astype(jnp.float32).astype(jnp.bfloat16)  108 us
    scatter-add x1, other arithmetic, on_device(): jnp.zeros((2, blocks * head_count, BS, DH), jnp.float32).at[:, recv_index]  51.8 us
    while x64, local copies, waits for them, and re-layouts  45.7 us
    psum x1, waiting for transfers between devices, on_device(): glob_sum = lax.psum(jnp.stack([results[5], results[6]]), 'seq')  39.9 us
    scatter x2, local copies, waits for them, and re-layouts, on_device(): jnp.zeros((2, spill_slot, BS, DH), jnp.bfloat16).at[:, send_pos]  38.8 us
    another operation x11, other arithmetic  25.8 us
    scatter x1, local copies, waits for them, and re-layouts, on_device(): jnp.zeros((spill_slot + 1,), jnp.int32).at[target].set(local_of.reshape(-1))  23 us
  transfers between devices with their start and end apart: 11, of which 7 were waited for; matrix products, arithmetic and copies ran while one was open for 17% of the time, Pallas kernels for 0%

commit v1 on v0

v1 whole, which is shorter than its diff:
```python
import jax
import jax.numpy as jnp
from jax import lax
from jax.experimental import pallas as pl
from jax.experimental.pallas import tpu as pltpu
from jax.sharding import PartitionSpec as P

DH = 128
BS = 64
SCALE = DH**-0.5
X_GROUPS = [[z * 8 + x * 2 + c for x in range(4)] for z in range(4) for c in range(2)]
HEAD_GROUPS = [
    [(2 * zh + zl) * 8 + x * 2 + c for zl in range(2) for c in range(2)]
    for zh in range(2)
    for x in range(4)
]
MIRROR = [(s, (3 - s // 8) * 8 + s % 8) for s in range(32)]
NT = (((1,), (1,)), ((), ()))
TN = (((0,), (0,)), ((), ()))


def dot(a, b, dims):
    return lax.dot_general(a, b, dims, preferred_element_type=jnp.float32)


def attend_kernel(tab, edge, q_ref, g_ref, rd_ref, kv_ref, dq_ref, dkv_ref, acc_ref):
    acc_ref[...] = jnp.zeros_like(acc_ref)
    lane = lax.broadcasted_iota(jnp.int32, (1, 8 * BS), 1)
    eye = lax.broadcasted_iota(jnp.int32, (BS, BS), 0) == lax.broadcasted_iota(
        jnp.int32, (BS, BS), 1
    )

    def step(i, carry):
        slots = [tab[i * 8 + j] for j in range(8)]
        keys = jnp.concatenate([kv_ref[p] for p in slots], axis=0)
        values = jnp.concatenate([kv_ref[p + 8] for p in slots], axis=0)
        q = q_ref[i]
        g = g_ref[i]
        state = edge[i]
        gone = ((lane < BS) & (state == 1)) | (
            (lane >= 2 * BS) & (lane < 3 * BS) & (state == 2)
        )
        bias = jnp.where(gone, -jnp.inf, 0.0)
        scores = dot(q, keys, NT) * SCALE + bias
        peak = jnp.max(scores, axis=1, keepdims=True)
        e = jnp.exp(scores - peak)
        weights = e * (1.0 / jnp.sum(e, axis=1, keepdims=True))
        rd = jnp.sum(jnp.where(eye, rd_ref[pl.ds(i, 1), :], 0.0), axis=1, keepdims=True)
        ds = weights * (dot(g, values, NT) - rd)
        wb = weights.astype(jnp.bfloat16)
        dsb = ds.astype(jnp.bfloat16)
        dq_ref[i] = (dot(dsb, keys, (((1,), (0,)), ((), ()))) * SCALE).astype(jnp.bfloat16)
        dk = dot(dsb, q, TN) * SCALE
        dv = dot(wb, g, TN)
        for j, p in enumerate(slots):
            acc_ref[p] += dk[j * BS : (j + 1) * BS]
            acc_ref[p + 8] += dv[j * BS : (j + 1) * BS]
        return carry

    lax.fori_loop(0, 64, step, 0)
    dkv_ref[...] = acc_ref[...].astype(jnp.bfloat16)


def attend(tab, edge, q, g, rd, kv):
    vmem = pl.BlockSpec(memory_space=pltpu.VMEM)
    smem = pl.BlockSpec(memory_space=pltpu.SMEM)
    return pl.pallas_call(
        attend_kernel,
        out_shape=(
            jax.ShapeDtypeStruct((64, BS, DH), jnp.bfloat16),
            jax.ShapeDtypeStruct((512, BS, DH), jnp.bfloat16),
        ),
        in_specs=[smem, smem, vmem, vmem, vmem, vmem],
        out_specs=(vmem, vmem),
        scratch_shapes=[pltpu.VMEM((512, BS, DH), jnp.float32)],
        compiler_params=pltpu.CompilerParams(vmem_limit_bytes=60 * 1024 * 1024),
    )(tab, edge, q, g, rd, kv)


def place(block, zhi):
    z, x, c = block // 64, block // 16 % 4, block // 8 % 2
    near = z // 2 == zhi
    zlo = jnp.where(near, z % 2, (3 - z) % 2)
    slot = ((zlo * 2 + c) * 2 + jnp.where(near, 0, 1)) * 4 + x
    return slot * 16 + block % 8


def tables(random_blocks, global_blocks, z, x, c):
    zhi = z // 2
    mine = lax.dynamic_index_in_dim(random_blocks, x * 2 + zhi, 1, keepdims=False)
    mine = mine.reshape(4, 4, 2, 8, 3)
    mine = lax.dynamic_index_in_dim(mine, c, 2, keepdims=False)
    near = lax.dynamic_index_in_dim(mine, z, 0, keepdims=False)
    far = lax.dynamic_index_in_dim(mine, 3 - z, 0, keepdims=False)
    rand = jnp.stack([near, far]).reshape(64, 3)
    ids = jnp.arange(64, dtype=jnp.int32)
    zs = jnp.where(ids < 32, z, 3 - z)
    block = zs * 64 + ids // 8 % 4 * 16 + c * 8 + ids % 8
    window = jnp.stack([block - 1, block, block + 1], axis=1)
    window = jnp.clip(window, 0, 255)
    globs = jnp.broadcast_to(global_blocks[None], (64, 2))
    table = place(jnp.concatenate([window, rand, globs], axis=1), zhi)
    edge = jnp.where(block == 0, 1, jnp.where(block == 255, 2, 0))
    return table.reshape(512), edge


def on_device(
    queries, key_states, value_states, forward_out, grad_out, random_blocks, global_blocks
):
    s = lax.axis_index("seq")
    z, x, c = s // 8, s // 2 % 4, s % 2
    zhi = z // 2
    tab, edge = tables(random_blocks, global_blocks, z, x, c)
    row_dot = jnp.sum(
        (grad_out.astype(jnp.float32) * forward_out.astype(jnp.float32)).reshape(512, 8, DH),
        axis=2,
    )

    def over_x(a):
        return lax.all_to_all(a, "seq", 0, 0, axis_index_groups=X_GROUPS, tiled=True)

    def to_head(a):
        own = lax.dynamic_index_in_dim(a, zhi, 0, keepdims=False)
        other = lax.dynamic_index_in_dim(a, 1 - zhi, 0, keepdims=False)
        return jnp.stack([own, lax.ppermute(other, "seq", MIRROR)])

    kv = jnp.stack([key_states, value_states]).reshape(2, 512, 4, 2, DH).transpose(2, 3, 0, 1, 4)
    kv = to_head(over_x(kv).transpose(1, 0, 2, 3, 4))
    kv = lax.all_gather(kv, "seq", axis_index_groups=HEAD_GROUPS)
    qg = jnp.stack([queries, grad_out]).reshape(2, 512, 4, 2, DH).transpose(2, 3, 0, 1, 4)
    qg = to_head(over_x(qg).transpose(1, 2, 0, 3, 4))
    rd = to_head(over_x(row_dot.T.reshape(4, 2, 512)).transpose(1, 0, 2))
    dq, dkv = attend(
        tab,
        edge,
        qg[:, 0].reshape(64, BS, DH),
        qg[:, 1].reshape(64, BS, DH),
        rd.reshape(64, BS),
        kv.reshape(512, BS, DH),
    )
    dkv = lax.psum_scatter(
        dkv.reshape(4, 2, 4, 2, 512, DH), "seq", axis_index_groups=HEAD_GROUPS
    )
    full = jnp.concatenate([dq.reshape(2, 4, 1, 512, DH), dkv], axis=2)
    near, far = full[0], lax.ppermute(full[1], "seq", MIRROR)
    low = zhi == 0
    both = jnp.stack([jnp.where(low, near, far), jnp.where(low, far, near)], axis=3)
    rows = over_x(both.reshape(4, 3, 512, 2 * DH)).transpose(1, 2, 0, 3).reshape(3, 512, 1024)
    outs = lax.all_to_all(rows, "head", split_axis=1, concat_axis=2, tiled=True)
    return outs[0], outs[1], outs[2]


def solution(mesh):
    return jax.shard_map(
        on_device,
        mesh=mesh,
        in_specs=(
            P("seq", "head"),
            P("seq", "head"),
            P("seq", "head"),
            P("seq", "head"),
            P("seq", "head"),
            P(None, "head", None),
            P(),
        ),
        out_specs=(P(("seq", "head"), None), P(("seq", "head"), None), P(("seq", "head"), None)),
        check_vma=False,
    )
```

time: 869 us -> 460 us (0.53); the launches traced: 853 us -> 455 us
  local copies, waits for them, and re-layouts: 277 us -> 53.4 us
  waiting for transfers between devices: 341 us -> 214 us
  other arithmetic: 132 us -> 16.3 us
  blocking collectives: 0 us -> 90.8 us
  Pallas kernels: 0 us -> 49.1 us
  matrix products: 47.9 us -> 0 us
  starting transfers between devices: 38.3 us -> 17.5 us
    psum x2 -> x0, waiting for transfers between devices: 148 us -> none  [the longest x1 108 us: on_device(): glob_kv = lax.psum(picked, 'seq').astype(jnp.float32).astype(jnp.bfloat16)]
    scatter x5 -> x0, local copies, waits for them, and re-layouts: 108 us -> none  [the longest x2 38.8 us: on_device(): jnp.zeros((2, spill_slot, BS, DH), jnp.bfloat16).at[:, send_pos]]
    ppermute x4, waiting for transfers between devices: 174 us -> 73 us  [the longest x3 38.3 us: to_head(): return jnp.stack([own, lax.ppermute(other, 'seq', MIRROR)])]
    all_to_all x0 -> x2, blocking collectives: none -> 90.8 us  [the longest x1 50.5 us: on_device(): outs = lax.all_to_all(rows, 'head', split_axis=1, concat_axis=2, tiled=True)]
    reduce_scatter x0 -> x1, waiting for transfers between devices: none -> 78.2 us  [on_device(): lax.psum_scatter(dkv.reshape(4, 2, 4, 2, 512, DH), 'seq', axis_index_grou...]
    scatter-add x3 -> x0, other arithmetic: 55.8 us -> none  [the longest x1 51.8 us: on_device(): jnp.zeros((2, blocks * head_count, BS, DH), jnp.float32).at[:, recv_index]]
    while x67 -> x0, local copies, waits for them, and re-layouts: 50.7 us -> none
    pallas_call x0 -> x1, Pallas kernels: none -> 49.1 us  [attend(): pl.pallas_call(attend_kernel, out_shape=(jax.ShapeDtypeStruct((64, BS, DH...]
  transfers between devices with their start and end apart: 11 -> 9, of which waited for: 7 -> 8; matrix products, arithmetic and copies ran while one was open for 17% -> 4% of each run, Pallas kernels for 0% -> 0%
where the time goes in v1:
time: 460 us; the launch traced here: 455 us
  waiting for transfers between devices  214 us (47%)
  blocking collectives  90.8 us (20%)
  local copies, waits for them, and re-layouts  53.4 us (12%)
  Pallas kernels  49.1 us (11%)
  starting transfers between devices  17.5 us (4%)
  other arithmetic  16.3 us (4%)
  between operations  14.3 us (3%)
    reduce_scatter x1, waiting for transfers between devices, on_device(): lax.psum_scatter(dkv.reshape(4, 2, 4, 2, 512, DH), 'seq', axis_index_grou...  78.2 us
    all_to_all x1, blocking collectives, on_device(): outs = lax.all_to_all(rows, 'head', split_axis=1, concat_axis=2, tiled=True)  50.5 us
    pallas_call x1, Pallas kernels, attend(): pl.pallas_call(attend_kernel, out_shape=(jax.ShapeDtypeStruct((64, BS, DH...  49.1 us
    all_to_all x3, waiting for transfers between devices, over_x(): lax.all_to_all(a, 'seq', 0, 0, axis_index_groups=X_GROUPS, tiled=True)  43.1 us
    all_to_all x1, blocking collectives, over_x(): lax.all_to_all(a, 'seq', 0, 0, axis_index_groups=X_GROUPS, tiled=True)  40.2 us
    ppermute x3, waiting for transfers between devices, to_head(): return jnp.stack([own, lax.ppermute(other, 'seq', MIRROR)])  38.3 us
    ppermute x1, waiting for transfers between devices, on_device(): near, far = (full[0], lax.ppermute(full[1], 'seq', MIRROR))  34.7 us
    all_gather x1, waiting for transfers between devices, on_device(): kv = lax.all_gather(kv, 'seq', axis_index_groups=HEAD_GROUPS)  19.8 us
  transfers between devices with their start and end apart: 9, of which 8 were waited for; matrix products, arithmetic and copies ran while one was open for 4% of the time, Pallas kernels for 0%

profile of v1, /device:TPU:33, one launch (start us, length us, event | category | flops | bytes accessed | tf_op | source)
XLA Modules:
  0.0 455.4 jit_solution(10476983993784611147)
XLA Ops:
  7.2 1.6 copy.69
  8.8 1.3 copy.70
  10.1 1.4 maximum_bitcast_fusion.1
  11.5 3.8 copy.71
  15.3 4.0 all-to-all-start.2
  19.3 25.5 %all-to-all-done.2 = bf16[4,2,2,512,128]{4,1,3,2,0:T(2,128)(2,1)S(1)} async-done(((bf16[4,2,2,512,128]{4,1,3,2,0:T(2,128)(2,1)}), bf16[4,2,2,512,128]{4,1,3,2,0:T(2,128)(2,1)S(1)}, u32[]{:S(2)}, u32[]{:S(2)}) %all-to-all-start.2) | async-done | bytes 2097184 | tf_op jit(solution)/shard_map/all_to_all | solution.py:120
  44.8 4.9 %constant_dynamic-slice_fusion.1 = (bf16[4,1,2,512,128]{4,1,3,2,0:T(2,128)(2,1)S(1)}, bf16[4,1,2,512,128]{4,1,3,2,0:T(2,128)(2,1)S(1)}) fusion(bf16[4,2,2,512,128]{4,1,3,2,0:T(2,128)(2,1)S(1)} %all-to-all-done.2, s32[]{:T(128)S(6)} %select_n.251, s32[]{:T(128)S(6)} %select_n.252), kind=kLoop, calls=%fused_computation.53 | loop fusion | bytes 4194312 | tf_op jit(solution)/shard_map/dynamic-slice.6
  49.7 0.2 copy.96
  49.8 1.7 collective-permute-start.2
  51.6 0.2 copy.97
  51.7 21.5 %collective-permute-done.2 = bf16[4,2,512,128]{3,2,1,0:T(8,128)(2,1)S(1)} collective-permute-done((bf16[4,2,512,128]{3,2,1,0:T(8,128)(2,1)S(1)}, bf16[4,2,512,128]{3,2,1,0:T(8,128)(2,1)S(1)}, u32[]{:S(2)}, u32[]{:S(2)}) %collective-permute-start.2) | collective-permute-done | bytes 1048608 | tf_op jit(solution)/shard_map/ppermute | solution.py:125
  73.2 1.6 pad_maximum_fusion.1
  74.8 1.2 copy-done.5
  76.0 1.3 copy.64
  77.3 1.3 copy.65
  78.6 1.7 maximum_bitcast_fusion
  80.4 2.4 copy.66
  82.7 3.7 all-to-all-start
  86.6 0.1 pad.16.clone
  86.7 0.1 reshape.178
  86.8 0.1 reshape.179
  86.9 1.7 multiply_bitcast_fusion
  88.7 1.8 copy.91
  90.5 2.4 reduce_sum.9
  92.9 0.1 copy.68
  93.0 0.6 reshape.181
  93.6 16.7 %all-to-all-done = bf16[4,2,2,512,128]{4,3,2,1,0:T(8,128)(2,1)S(1)} async-done(((bf16[4,2,2,512,128]{4,3,2,1,0:T(8,128)(2,1)}), bf16[4,2,2,512,128]{4,3,2,1,0:T(8,128)(2,1)S(1)}, u32[]{:S(2)}, u32[]{:S(2)}) %all-to-all-start) | async-done | bytes 2097184 | tf_op jit(solution)/shard_map/all_to_all | solution.py:120
  110.3 3.3 all-to-all-start.1
  113.6 0.0 reduce-scatter.2.cloned.1.call-start
  113.6 1.1 dynamic-slice_bitcast_fusion
  114.8 1.1 collective-permute-start
  115.9 0.1 add_add_fusion
  116.0 0.1 copy.63
  116.1 0.1 concatenate.11
  116.1 0.6 fusion.17.tab
  116.8 1.0 all-to-all-done.1
  117.8 1.4 collective-permute-start.1
  119.2 0.6 compare_select_fusion.5.edge
  119.8 16.8 %collective-permute-done.1 = f32[4,512]{1,0:T(4,128)S(1)} collective-permute-done((f32[4,512]{1,0:T(4,128)S(1)}, f32[4,512]{1,0:T(4,128)S(1)}, u32[]{:S(2)}, u32[]{:S(2)}) %collective-permute-start.1) | collective-permute-done | bytes 8224 | tf_op jit(solution)/shard_map/ppermute | solution.py:125
  136.6 0.7 reshape.182.rd_ref
  137.3 1.5 pad_maximum_fusion.3
  138.8 19.8 %all-gather.3.cloned.1.call-done = bf16[8,4,2,512,128]{4,3,2,1,0:T(8,128)(2,1)} async-done(((bf16[2,4,2,512,128]{4,3,2,1,0:T(8,128)(2,1)}), bf16[8,4,2,512,128]{4,3,2,1,0:T(8,128)(2,1)}) %all-gather.3.cloned.1.call-update) | async-done | bytes 8388624 | tf_op jit(solution)/shard_map/all_gather | solution.py:129
  158.5 49.1 %shard_map.94 = (bf16[64,64,128]{2,1,0:T(8,128)(2,1)}, bf16[512,64,128]{2,1,0:T(8,128)(2,1)}) custom-call(s32[512]{0:T(512)} %fusion.17.tab, s32[64]{0:T(128)} %compare_select_fusion.5.edge, bf16[64,64,128]{2,1,0:T(8,128)(2,1)} %bitcast.80, bf16[64,64,128]{2,1,0:T(8,128)(2,1)} %bitcast.79, f32[64,64]{1,0:T(8,128)} %reshape.182.rd_ref, ...), custom_call_target="tpu_custom_call" | custom-call | tf_op jit(solution)/shard_map/pallas_call | solution.py:67
  207.6 13.2 %copy.74 = bf16[4,2,4,2,512,128]{4,5,3,2,1,0:T(8,128)(2,1)} copy(bf16[4,2,4,2,512,128]{5,4,3,2,1,0:T(8,128)(2,1)} %bitcast.76) | data formatting | bytes 16777216 | tf_op jit(solution)/shard_map/reshape | solution.py:142
  220.8 1.2 copy-done.6
  222.0 0.5 copy.75
  222.6 78.2 %reduce-scatter.2.cloned.1.call-done = bf16[1,2,4,2,512,128]{4,5,3,2,1,0:T(8,128)(2,1)} async-done(((bf16[4,2,4,2,512,128]{4,5,3,2,1,0:T(8,128)(2,1)}), bf16[1,2,4,2,512,128]{4,5,3,2,1,0:T(8,128)(2,1)}) %reduce-scatter.2.cloned.1.call-update) | async-done | bytes 2097168 | tf_op jit(solution)/shard_map/reduce_scatter | solution.py:141
  300.8 2.7 fusion.2
  303.5 2.3 collective-permute-start.3
  305.7 34.7 %collective-permute-done.3 = bf16[4,3,512,128]{2,3,1,0:T(8,128)(2,1)} collective-permute-done((bf16[4,3,512,128]{2,3,1,0:T(8,128)(2,1)}, bf16[4,3,512,128]{2,3,1,0:T(8,128)(2,1)}, u32[]{:S(2)}, u32[]{:S(2)}) %collective-permute-start.3) | collective-permute-done | bytes 1572896 | tf_op jit(solution)/shard_map/ppermute | solution.py:145
  340.5 1.6 select_bitcast_fusion.1
  342.0 0.3 pad_maximum_fusion
  342.3 40.2 %all_to_all.35 = bf16[4,3,512,256]{2,3,1,0:T(8,128)(2,1)S(1)} all-to-all(bf16[4,3,512,256]{2,3,1,0:T(8,128)(2,1)S(1)} %bitcast.72), channel_id=1, replica_groups={{0,8,16,24},{4,12,20,28},{32,40,48,56},{36,44,52,60},{64,72,80,88},{68,..., dimensions={0} | all-to-all | bytes 6291456 | tf_op jit(solution)/shard_map/all_to_all | solution.py:120
  382.6 0.4 copy.77
  383.0 5.6 %copy.78 = bf16[3,512,1024]{2,0,1:T(4,128)(2,1)} copy(bf16[3,512,1024]{1,2,0:T(8,128)(2,1)S(1)} %bitcast.71) | data formatting | bytes 6291456 | tf_op jit(solution)/shard_map/reshape | solution.py:148
  388.6 50.5 %all_to_all.36 = bf16[3,512,1024]{2,0,1:T(4,128)(2,1)S(1)} all-to-all(bf16[3,512,1024]{2,0,1:T(4,128)(2,1)} %copy.78), channel_id=1, replica_groups=mesh['seq'=32,'head'=4] {'head'}, dimensions={1} | all-to-all | bytes 6291456 | tf_op jit(solution)/shard_map/all_to_all | solution.py:149
  439.1 1.2 copy.79
  440.4 1.3 fusion.33
  441.7 1.6 copy.82
  443.3 1.3 copy.85
  444.6 0.7 copy.81
  445.3 1.3 copy.84
  446.6 0.7 copy.80
  447.3 1.3 copy.83
  (29 shorter events, 0.2 us)
Async XLA Ops:
  7.2 79.5 %copy-start = (s32[256,8,3]{0,1,2:T(8,128)S(1)}, s32[256,8,3]{0,1,2:T(8,128)}, u32[]{:S(2)}) copy-start(s32[256,8,3]{0,1,2:T(8,128)} %param.12) | copy-start | bytes 73732
  7.2 1.6 copy-start.4
  15.3 29.5 %all-to-all-start.2 = ((bf16[4,2,2,512,128]{4,1,3,2,0:T(2,128)(2,1)}), bf16[4,2,2,512,128]{4,1,3,2,0:T(2,128)(2,1)S(1)}, u32[]{:S(2)}, u32[]{:S(2)}) async-start(bf16[4,2,2,512,128]{4,1,3,2,0:T(2,128)(2,1)} %copy.71), calls=%async_computation.2 | async-start | bytes 4194304 | tf_op jit(solution)/shard_map/all_to_all | solution.py:120
  19.3 139.2 %all-gather.3.cloned.1.call-start = ((), (), s32[]{:S(2)}) async-start(), calls=%async_computation.7 | async-start | bytes 10485760 | tf_op jit(solution)/shard_map/all_gather | solution.py:129
  49.8 23.3 %collective-permute-start.2 = (bf16[4,2,512,128]{3,2,1,0:T(8,128)(2,1)S(1)}, bf16[4,2,512,128]{3,2,1,0:T(8,128)(2,1)S(1)}, u32[]{:S(2)}, u32[]{:S(2)}) collective-permute-start(bf16[4,2,512,128]{3,2,1,0:T(8,128)(2,1)S(1)} %bitcast.89), channel_id=1, source_target_pairs={{0,96},{4,100},{8,104},{12,108},{16,112},{20,116},{24,120},{28,124... | collective-permute-start | bytes 3145736 | tf_op jit(solution)/shard_map/ppermute | solution.py:125
  74.8 1.2 copy-start.5
  74.8 2.5 copy-start.3
  82.7 3.8 copy-start.7
  82.7 27.6 %all-to-all-start = ((bf16[4,2,2,512,128]{4,3,2,1,0:T(8,128)(2,1)}), bf16[4,2,2,512,128]{4,3,2,1,0:T(8,128)(2,1)S(1)}, u32[]{:S(2)}, u32[]{:S(2)}) async-start(bf16[4,2,2,512,128]{4,3,2,1,0:T(8,128)(2,1)} %copy.66), calls=%async_computation | async-start | bytes 4194304 | tf_op jit(solution)/shard_map/all_to_all | solution.py:120
  110.3 7.4 %all-to-all-start.1 = ((f32[4,2,512]{2,1,0:T(2,128)}), f32[4,2,512]{2,1,0:T(2,128)S(1)}, u32[]{:S(2)}, u32[]{:S(2)}) async-start(f32[4,2,512]{2,1,0:T(2,128)} %reshape.181), calls=%async_computation.1 | async-start | bytes 32768 | tf_op jit(solution)/shard_map/all_to_all | solution.py:120
  113.6 187.2 %reduce-scatter.2.cloned.1.call-start = ((), (), s32[]{:S(2)}) async-start(), calls=%async_computation.6 | async-start | bytes 10485760 | tf_op jit(solution)/shard_map/reduce_scatter | solution.py:141
  114.8 22.5 %collective-permute-start = (bf16[2,4,512,128]{3,2,0,1:T(8,128)(2,1)}, bf16[2,4,512,128]{3,2,0,1:T(8,128)(2,1)S(1)}, u32[]{:S(2)}, u32[]{:S(2)}) collective-permute-start(bf16[2,4,512,128]{3,2,0,1:T(8,128)(2,1)} %get-tuple-element.27), channel_id=1, source_target_pairs={{0,96},{4,100},{8,104},{12,108},{16,112},{20,116},{24,120},{28,124... | collective-permute-start | bytes 3145736 | tf_op jit(solution)/shard_map/ppermute | solution.py:125
  117.8 18.8 %collective-permute-start.1 = (f32[4,512]{1,0:T(4,128)S(1)}, f32[4,512]{1,0:T(4,128)S(1)}, u32[]{:S(2)}, u32[]{:S(2)}) collective-permute-start(f32[4,512]{1,0:T(4,128)S(1)} %bitcast.97), channel_id=1, source_target_pairs={{0,96},{4,100},{8,104},{12,108},{16,112},{20,116},{24,120},{28,124... | collective-permute-start | bytes 24584 | tf_op jit(solution)/shard_map/ppermute | solution.py:125
  220.8 1.2 copy-start.6
  300.8 39.7 %copy-start.2 = (bf16[1,2,4,2,512,128]{4,5,3,2,1,0:T(8,128)(2,1)S(1)}, bf16[1,2,4,2,512,128]{4,5,3,2,1,0:T(8,128)(2,1)}, u32[]{:S(2)}) copy-start(bf16[1,2,4,2,512,128]{4,5,3,2,1,0:T(8,128)(2,1)} %reduce-scatter.2.cloned.1.call-done) | copy-start | bytes 6291460
  303.5 37.0 %collective-permute-start.3 = (bf16[4,3,512,128]{2,3,1,0:T(8,128)(2,1)}, bf16[4,3,512,128]{2,3,1,0:T(8,128)(2,1)}, u32[]{:S(2)}, u32[]{:S(2)}) collective-permute-start(bf16[4,3,512,128]{2,3,1,0:T(8,128)(2,1)} %fusion.2), channel_id=1, source_target_pairs={{0,96},{4,100},{8,104},{12,108},{16,112},{20,116},{24,120},{28,124... | collective-permute-start | bytes 4718600 | tf_op jit(solution)/shard_map/ppermute | solution.py:145
  446.6 2.0 copy-start.1
Sparse Core Ops, SparseCore 0:
  74.9 83.5 all-gather.2
  221.0 79.7 reduce-scatter.1

commit v2 on v1

--- a/solution.py
+++ b/solution.py
@@ -23,7 +23,204 @@
     return lax.dot_general(a, b, dims, preferred_element_type=jnp.float32)
 
 
-def attend_kernel(tab, edge, q_ref, g_ref, rd_ref, kv_ref, dq_ref, dkv_ref, acc_ref):
+MESH = pl.DeviceIdType.MESH
+
+
+def fetch_kernel(
+    k_ref, v_ref, q_ref, g_ref, rd_ref,
+    kv_out, qg_out, rdx, rdm,
+    loc, oth, hop,
+    send, local, from_x, from_2, from_hop, from_pair, from_mirror, from_core, from_rd,
+):
+    s = lax.axis_index("seq")
+    z, x, c = s // 8, s // 2 % 4, s % 2
+    zhi = z // 2
+    mirror, pair, core = 3 - z, z + 1 - 2 * (z % 2), 1 - c
+
+    def index(zz, xx, cc):
+        return zz * 8 + xx % 4 * 2 + cc
+
+    to_mirror, to_pair, to_core = index(mirror, x, c), index(pair, x, c), index(z, x, core)
+    barrier = pltpu.get_barrier_semaphore()
+    greet = [index(z, x + d, c) for d in (1, 2, 3)] + [to_mirror, to_pair, to_core]
+    for peer in greet:
+        pl.semaphore_signal(barrier, inc=1, device_id={"seq": peer}, device_id_type=MESH)
+    pl.semaphore_wait(barrier, len(greet))
+
+    sends = []
+
+    def push(src, dst, sem, peer):
+        copy = pltpu.make_async_remote_copy(
+            src_ref=src,
+            dst_ref=dst,
+            send_sem=send.at[len(sends)],
+            recv_sem=sem,
+            device_id={"seq": peer},
+            device_id_type=MESH,
+        )
+        copy.start()
+        sends.append(copy)
+
+    def arrived(dst, sem):
+        pltpu.make_async_remote_copy(
+            src_ref=dst,
+            dst_ref=dst,
+            send_sem=send.at[0],
+            recv_sem=sem,
+            device_id={"seq": to_core},
+            device_id_type=MESH,
+        ).wait_recv()
+
+    locals_ = []
+
+    def move(src, dst):
+        copy = pltpu.make_async_copy(src, dst, local.at[len(locals_)])
+        copy.start()
+        locals_.append(copy)
+        return copy
+
+    ins = (k_ref, v_ref, q_ref, g_ref)
+
+    def own(a, xx):
+        return ins[a].at[:, pl.ds(pl.multiple_of(xx % 4 * 256 + zhi * DH, DH), DH)]
+
+    def other(a, xx):
+        return ins[a].at[:, pl.ds(pl.multiple_of(xx % 4 * 256 + (1 - zhi) * DH, DH), DH)]
+
+    def own_slot(a, src_s, src_x):
+        return kv_out.at[src_s, a] if a < 2 else qg_out.at[src_x, a - 2]
+
+    def send_x(arrays):
+        for a in arrays:
+            push(own(a, x + 2), hop.at[0, a], from_hop.at[0, a], index(z, x + 1, c))
+            push(other(a, x + 2), hop.at[1, a], from_hop.at[1, a], index(z, x + 3, c))
+            for d in (1, 3):
+                peer = index(z, x + d, c)
+                push(own(a, x + d), own_slot(a, s, x), from_x.at[d // 2, a, 0], peer)
+                push(other(a, x + d), oth.at[x, a], from_x.at[d // 2, a, 1], peer)
+
+    def relay(pair_of, base):
+        for a in pair_of:
+            arrived(hop.at[0, a], from_hop.at[0, a])
+        left, right = (x + 3) % 4, (x + 1) % 4
+        both = pl.ds(base, 2)
+        dst = kv_out.at[index(z, left, c)] if base == 0 else qg_out.at[left]
+        push(hop.at[0, both], dst, from_2.at[base], index(z, right, c))
+        for a in pair_of:
+            arrived(hop.at[1, a], from_hop.at[1, a])
+        push(hop.at[1, both], oth.at[right, both], from_2.at[base + 1], index(z, left, c))
+
+    loads = [[move(own(a, x), loc.at[a]), move(other(a, x), oth.at[x, a])] for a in range(4)]
+    rd_load = move(rd_ref.at[x], rdx.at[x])
+    send_x((0, 1))
+    for d in (1, 2, 3):
+        push(rd_ref.at[(x + d) % 4], rdx.at[x], from_rd.at[d], index(z, x + d, c))
+    for a in (0, 1):
+        loads[a][0].wait()
+        loads[a][1].wait()
+    kv = pl.ds(0, 2)
+    qg = pl.ds(2, 2)
+    push(loc.at[kv], kv_out.at[s], from_pair.at[0, 0], to_pair)
+    push(oth.at[x, kv], kv_out.at[s], from_mirror.at[0, 0], to_mirror)
+    push(loc.at[kv], kv_out.at[s], from_core.at[0, 0], to_core)
+    stores = [move(loc.at[kv], kv_out.at[s])]
+    send_x((2, 3))
+    for a in (2, 3):
+        loads[a][0].wait()
+        loads[a][1].wait()
+    stores.append(move(loc.at[qg], qg_out.at[x]))
+    relay((0, 1), 0)
+    for r in (3, 1, 2):
+        src = (x + r) % 4
+        slot = index(z, src, c)
+        if r == 2:
+            arrived(kv_out.at[slot], from_2.at[0])
+        else:
+            for a in (0, 1):
+                arrived(kv_out.at[slot, a], from_x.at[(4 - r) // 2, a, 0])
+        push(kv_out.at[slot], kv_out.at[slot], from_pair.at[0, r], to_pair)
+        if r == 2:
+            arrived(oth.at[src, kv], from_2.at[1])
+        else:
+            for a in (0, 1):
+                arrived(oth.at[src, a], from_x.at[(4 - r) // 2, a, 1])
+        push(oth.at[src, kv], kv_out.at[slot], from_mirror.at[0, r], to_mirror)
+        push(kv_out.at[slot], kv_out.at[slot], from_core.at[0, r], to_core)
+    push(oth.at[x, qg], qg_out.at[4 + x], from_mirror.at[1, 0], to_mirror)
+    for r in (0, 3, 1, 2):
+        slot = index(mirror, x + r, c)
+        arrived(kv_out.at[slot], from_mirror.at[0, r])
+        push(kv_out.at[slot], kv_out.at[slot], from_pair.at[1, r], to_pair)
+        push(kv_out.at[slot], kv_out.at[slot], from_core.at[1, r], to_core)
+    relay((2, 3), 2)
+    for r in (3, 1, 2):
+        src = (x + r) % 4
+        if r == 2:
+            arrived(oth.at[src, qg], from_2.at[3])
+        else:
+            for a in (2, 3):
+                arrived(oth.at[src, a], from_x.at[(4 - r) // 2, a, 1])
+        push(oth.at[src, qg], qg_out.at[4 + src], from_mirror.at[1, r], to_mirror)
+    rd_load.wait()
+    for d in (1, 2, 3):
+        arrived(rdx.at[(x + 4 - d) % 4], from_rd.at[d])
+    push(rdx, rdm, from_rd.at[0], to_mirror)
+    for m, zz in ((0, pair), (1, 3 - pair)):
+        for r in (0, 3, 1, 2):
+            slot = index(zz, x + r, c)
+            arrived(kv_out.at[slot], from_pair.at[m, r])
+            push(kv_out.at[slot], kv_out.at[slot], from_core.at[2 + m, r], to_core)
+    for r in (3, 1, 2):
+        src = (x + r) % 4
+        if r == 2:
+            arrived(qg_out.at[src], from_2.at[2])
+        else:
+            for a in (2, 3):
+                arrived(qg_out.at[src, a - 2], from_x.at[(4 - r) // 2, a, 0])
+    for r in range(4):
+        arrived(qg_out.at[4 + (x + r) % 4], from_mirror.at[1, r])
+        for m, zz in enumerate((z, mirror, pair, 3 - pair)):
+            arrived(kv_out.at[index(zz, x + r, core)], from_core.at[m, r])
+    arrived(rdm, from_rd.at[0])
+    for copy in stores:
+        copy.wait()
+    for copy in sends:
+        copy.wait_send()
+
+
+def fetch(k, v, q, g, rd):
+    anywhere = pl.BlockSpec(memory_space=pl.ANY)
+    vmem = pl.BlockSpec(memory_space=pltpu.VMEM)
+    dma = pltpu.SemaphoreType.DMA
+    return pl.pallas_call(
+        fetch_kernel,
+        out_shape=(
+            jax.ShapeDtypeStruct((32, 2, 512, DH), jnp.bfloat16),
+            jax.ShapeDtypeStruct((8, 2, 512, DH), jnp.bfloat16),
+            jax.ShapeDtypeStruct((4, 8, 128), jnp.float32),
+            jax.ShapeDtypeStruct((4, 8, 128), jnp.float32),
+        ),
+        in_specs=[anywhere] * 5,
+        out_specs=(anywhere, anywhere, vmem, vmem),
+        scratch_shapes=[
+            pltpu.VMEM((4, 512, DH), jnp.bfloat16),
+            pltpu.VMEM((4, 4, 512, DH), jnp.bfloat16),
+            pltpu.VMEM((2, 4, 512, DH), jnp.bfloat16),
+            dma((80,)),
+            dma((12,)),
+            dma((2, 4, 2)),
+            dma((4,)),
+            dma((2, 4)),
+            dma((2, 4)),
+            dma((2, 4)),
+            dma((4, 4)),
+            dma((4,)),
+        ],
+        compiler_params=pltpu.CompilerParams(collective_id=0, has_side_effects=True),
+    )(k, v, q, g, rd)
+
+
+def attend_kernel(tab, edge, acc_tab, qg_ref, rd_ref, kv_ref, dq_ref, dkv_ref, acc_ref):
     acc_ref[...] = jnp.zeros_like(acc_ref)
     lane = lax.broadcasted_iota(jnp.int32, (1, 8 * BS), 1)
     eye = lax.broadcasted_iota(jnp.int32, (BS, BS), 0) == lax.broadcasted_iota(
@@ -32,10 +229,12 @@
 
     def step(i, carry):
         slots = [tab[i * 8 + j] for j in range(8)]
+        acc_slots = [acc_tab[i * 8 + j] for j in range(8)]
+        at = i // 8 * 16 + i % 8
         keys = jnp.concatenate([kv_ref[p] for p in slots], axis=0)
         values = jnp.concatenate([kv_ref[p + 8] for p in slots], axis=0)
-        q = q_ref[i]
-        g = g_ref[i]
+        q = qg_ref[at]
+        g = qg_ref[at + 8]
         state = edge[i]
         gone = ((lane < BS) & (state == 1)) | (
             (lane >= 2 * BS) & (lane < 3 * BS) & (state == 2)
@@ -52,7 +251,7 @@
         dq_ref[i] = (dot(dsb, keys, (((1,), (0,)), ((), ()))) * SCALE).astype(jnp.bfloat16)
         dk = dot(dsb, q, TN) * SCALE
         dv = dot(wb, g, TN)
-        for j, p in enumerate(slots):
+        for j, p in enumerate(acc_slots):
             acc_ref[p] += dk[j * BS : (j + 1) * BS]
             acc_ref[p + 8] += dv[j * BS : (j + 1) * BS]
         return carry
@@ -61,7 +260,7 @@
     dkv_ref[...] = acc_ref[...].astype(jnp.bfloat16)
 
 
-def attend(tab, edge, q, g, rd, kv):
+def attend(tab, edge, acc_tab, qg, rd, kv):
     vmem = pl.BlockSpec(memory_space=pltpu.VMEM)
     smem = pl.BlockSpec(memory_space=pltpu.SMEM)
     return pl.pallas_call(
@@ -70,11 +269,11 @@
             jax.ShapeDtypeStruct((64, BS, DH), jnp.bfloat16),
             jax.ShapeDtypeStruct((512, BS, DH), jnp.bfloat16),
         ),
-        in_specs=[smem, smem, vmem, vmem, vmem, vmem],
+        in_specs=[smem, smem, smem, vmem, vmem, vmem],
         out_specs=(vmem, vmem),
         scratch_shapes=[pltpu.VMEM((512, BS, DH), jnp.float32)],
         compiler_params=pltpu.CompilerParams(vmem_limit_bytes=60 * 1024 * 1024),
-    )(tab, edge, q, g, rd, kv)
+    )(tab, edge, acc_tab, qg, rd, kv)
 
 
 def place(block, zhi):
@@ -99,9 +298,11 @@
     window = jnp.stack([block - 1, block, block + 1], axis=1)
     window = jnp.clip(window, 0, 255)
     globs = jnp.broadcast_to(global_blocks[None], (64, 2))
-    table = place(jnp.concatenate([window, rand, globs], axis=1), zhi)
+    table = jnp.concatenate([window, rand, globs], axis=1)
+    acc_table = place(table, zhi)
+    table = table // 8 * 16 + table % 8
     edge = jnp.where(block == 0, 1, jnp.where(block == 255, 2, 0))
-    return table.reshape(512), edge
+    return table.reshape(512), edge, acc_table.reshape(512)
 
 
 def on_device(
@@ -110,7 +311,7 @@
     s = lax.axis_index("seq")
     z, x, c = s // 8, s // 2 % 4, s % 2
     zhi = z // 2
-    tab, edge = tables(random_blocks, global_blocks, z, x, c)
+    tab, edge, acc_tab = tables(random_blocks, global_blocks, z, x, c)
     row_dot = jnp.sum(
         (grad_out.astype(jnp.float32) * forward_out.astype(jnp.float32)).reshape(512, 8, DH),
         axis=2,
@@ -119,22 +320,17 @@
     def over_x(a):
         return lax.all_to_all(a, "seq", 0, 0, axis_index_groups=X_GROUPS, tiled=True)
 
-    def to_head(a):
-        own = lax.dynamic_index_in_dim(a, zhi, 0, keepdims=False)
-        other = lax.dynamic_index_in_dim(a, 1 - zhi, 0, keepdims=False)
-        return jnp.stack([own, lax.ppermute(other, "seq", MIRROR)])
-
-    kv = jnp.stack([key_states, value_states]).reshape(2, 512, 4, 2, DH).transpose(2, 3, 0, 1, 4)
-    kv = to_head(over_x(kv).transpose(1, 0, 2, 3, 4))
-    kv = lax.all_gather(kv, "seq", axis_index_groups=HEAD_GROUPS)
-    qg = jnp.stack([queries, grad_out]).reshape(2, 512, 4, 2, DH).transpose(2, 3, 0, 1, 4)
-    qg = to_head(over_x(qg).transpose(1, 2, 0, 3, 4))
-    rd = to_head(over_x(row_dot.T.reshape(4, 2, 512)).transpose(1, 0, 2))
+    kv, qg, rdx, rdm = fetch(
+        key_states, value_states, queries, grad_out, row_dot.T.reshape(4, 8, 128)
+    )
+    rd = lax.dynamic_index_in_dim(
+        jnp.stack([rdx, rdm]).reshape(2, 4, 2, 512), zhi, 2, keepdims=False
+    )
     dq, dkv = attend(
         tab,
         edge,
-        qg[:, 0].reshape(64, BS, DH),
-        qg[:, 1].reshape(64, BS, DH),
+        acc_tab,
+        qg.reshape(128, BS, DH),
         rd.reshape(64, BS),
         kv.reshape(512, BS, DH),
     )

time: 460 us -> 394 us (0.86)
  waiting for transfers between devices: 214 us -> 110 us
  Pallas kernels: 49.1 us -> 129 us
  local copies, waits for them, and re-layouts: 53.4 us -> 34.9 us
  starting transfers between devices: 17.5 us -> 2.3 us
  other arithmetic: 16.3 us -> 8.4 us
    pallas_call x0 -> x1, Pallas kernels: none -> 79.5 us  [fetch(): pl.pallas_call(fetch_kernel, out_shape=(jax.ShapeDtypeStruct((32, 2, 512,...]
    all_to_all x3 -> x0, waiting for transfers between devices: 43.1 us -> none  [over_x(): lax.all_to_all(a, 'seq', 0, 0, axis_index_groups=X_GROUPS, tiled=True)]
    ppermute x3 -> x0, waiting for transfers between devices: 38.3 us -> none  [to_head(): return jnp.stack([own, lax.ppermute(other, 'seq', MIRROR)])]
    all_gather x1 -> x0, waiting for transfers between devices: 19.8 us -> none  [on_device(): kv = lax.all_gather(kv, 'seq', axis_index_groups=HEAD_GROUPS)]
    all_to_all x3 -> x0, starting transfers between devices: 11 us -> none  [over_x(): lax.all_to_all(a, 'seq', 0, 0, axis_index_groups=X_GROUPS, tiled=True)]
    unnamed x28 -> x12, local copies, waits for them, and re-layouts: 14 us -> 5.63 us
    transpose x3 -> x1, local copies, waits for them, and re-layouts: 6.24 us -> 0.09 us  [on_device(): row_dot.T.reshape(4, 8, 128)]
  transfers between devices with their start and end apart: 9 -> 2, of which waited for: 8 -> 2; matrix products, arithmetic and copies ran while one was open for 4% -> 0% of each run, Pallas kernels for 0% -> 0%
where the time goes in v2:
time: 394 us; the launch traced here: 389 us
  Pallas kernels  129 us (33%)
  waiting for transfers between devices  110 us (28%)
  blocking collectives  90.8 us (23%)
  local copies, waits for them, and re-layouts  34.9 us (9%)
  between operations  14.3 us (4%)
  other arithmetic  8.4 us (2%)
    pallas_call x1, Pallas kernels, fetch(): pl.pallas_call(fetch_kernel, out_shape=(jax.ShapeDtypeStruct((32, 2, 512,...  79.5 us
    reduce_scatter x1, waiting for transfers between devices, on_device(): lax.psum_scatter(dkv.reshape(4, 2, 4, 2, 512, DH), 'seq', axis_index_grou...  75.2 us
    all_to_all x1, blocking collectives, on_device(): outs = lax.all_to_all(rows, 'head', split_axis=1, concat_axis=2, tiled=True)  50.5 us
    pallas_call x1, Pallas kernels, attend(): pl.pallas_call(attend_kernel, out_shape=(jax.ShapeDtypeStruct((64, BS, DH...  49 us
    all_to_all x1, blocking collectives, over_x(): lax.all_to_all(a, 'seq', 0, 0, axis_index_groups=X_GROUPS, tiled=True)  40.3 us
    ppermute x1, waiting for transfers between devices, on_device(): near, far = (full[0], lax.ppermute(full[1], 'seq', MIRROR))  34.7 us
    reshape x1, local copies, waits for them, and re-layouts, on_device(): dkv.reshape(4, 2, 4, 2, 512, DH)  13.3 us
  transfers between devices with their start and end apart: 2, of which 2 were waited for; matrix products, arithmetic and copies ran while one was open for 0% of the time, Pallas kernels for 0%

profile of v2, /device:TPU:33, one launch (start us, length us, event | category | flops | bytes accessed | tf_op | source)
XLA Modules:
  0.0 389.2 jit_solution(359589691949643449)
XLA Ops:
  7.2 0.0 copy-start
  7.2 0.0 reduce-scatter.2.cloned.1.call-start
  7.3 0.6 compare_select_fusion.5.edge
  7.9 0.7 pad.8.clone
  8.7 0.0 copy-done
  8.7 0.1 reshape.173
  8.9 0.1 reshape.174
  9.0 0.1 add_add_fusion
  9.1 0.1 copy.38
  9.2 0.1 concatenate.10
  9.2 0.6 multiply_add_fusion
  9.9 1.9 multiply_bitcast_fusion
  11.8 0.5 copy.54
  12.3 0.6 reduce_sum.9
  12.9 0.1 copy.39
  13.0 0.6 reshape.176.rd_ref
  13.6 79.5 %shard_map.94 = (bf16[32,2,512,128]{3,2,1,0:T(8,128)(2,1)}, bf16[8,2,512,128]{3,2,1,0:T(8,128)(2,1)}, f32[4,8,128]{2,1,0:T(8,128)}, f32[4,8,128]{2,1,0:T(8,128)}) custom-call(bf16[512,1024]{1,0:T(8,128)(2,1)} %k_ref.1, bf16[512,1024]{1,0:T(8,128)(2,1)} %v_ref.1, bf16[512,1024]{1,0:T(8,128)(2,1)} %q_ref.1, bf16[512,1024]{1,0:T(8,128)(2,1)} %g_ref.1, ...), custom_call_target="tpu_custom_call" | custom-call | tf_op jit(solution)/shard_map/pallas_call | solution.py:195
  93.1 0.7 stack.31
  93.9 0.7 stack.32
  94.6 0.7 reshape.178.rd_ref
  95.3 49.0 %shard_map.95 = (bf16[64,64,128]{2,1,0:T(8,128)(2,1)}, bf16[512,64,128]{2,1,0:T(8,128)(2,1)}) custom-call(s32[512]{0:T(512)} %get-tuple-element.31.tab, s32[64]{0:T(128)} %compare_select_fusion.5.edge, s32[512]{0:T(512)} %get-tuple-element.30.acc_tab, bf16[128,64,128]{2,1,0:T(8,128)(2,1)} %bitcast.52, f32[64,64]{1,0:T(8,128)} %reshape.178.rd_ref, ...), custom_call_target="tpu_custom_call" | custom-call | tf_op jit(solution)/shard_map/pallas_call | solution.py:266
  144.4 13.3 %copy.42 = bf16[4,2,4,2,512,128]{4,5,3,2,1,0:T(8,128)(2,1)} copy(bf16[4,2,4,2,512,128]{5,4,3,2,1,0:T(8,128)(2,1)} %bitcast.46) | data formatting | bytes 16777216 | tf_op jit(solution)/shard_map/reshape | solution.py:338
  157.6 0.0 copy-start.3
  157.6 0.0 reduce-scatter.2.cloned.1.call-update
  157.7 1.2 copy-done.3
  158.9 0.5 copy.43
  159.4 75.2 %reduce-scatter.2.cloned.1.call-done = bf16[1,2,4,2,512,128]{4,5,3,2,1,0:T(8,128)(2,1)} async-done(((bf16[4,2,4,2,512,128]{4,5,3,2,1,0:T(8,128)(2,1)}), bf16[1,2,4,2,512,128]{4,5,3,2,1,0:T(8,128)(2,1)}) %reduce-scatter.2.cloned.1.call-update) | async-done | bytes 2097168 | tf_op jit(solution)/shard_map/reduce_scatter | solution.py:337
  234.6 0.0 copy-start.2
  234.6 2.7 fusion.2
  237.3 2.3 collective-permute-start
  239.5 34.7 %collective-permute-done = bf16[4,3,512,128]{2,3,1,0:T(8,128)(2,1)} collective-permute-done((bf16[4,3,512,128]{2,3,1,0:T(8,128)(2,1)}, bf16[4,3,512,128]{2,3,1,0:T(8,128)(2,1)}, u32[]{:S(2)}, u32[]{:S(2)}) %collective-permute-start) | collective-permute-done | bytes 1572896 | tf_op jit(solution)/shard_map/ppermute | solution.py:341
  274.3 0.0 copy-done.2
  274.3 1.6 select_bitcast_fusion.1
  275.8 0.3 pad_maximum_fusion
  276.1 40.3 %all_to_all.20 = bf16[4,3,512,256]{2,3,1,0:T(8,128)(2,1)S(1)} all-to-all(bf16[4,3,512,256]{2,3,1,0:T(8,128)(2,1)S(1)} %bitcast.42), channel_id=1, replica_groups={{0,8,16,24},{4,12,20,28},{32,40,48,56},{36,44,52,60},{64,72,80,88},{68,..., dimensions={0} | all-to-all | bytes 6291456 | tf_op jit(solution)/shard_map/all_to_all | solution.py:321
  316.4 0.4 copy.45
  316.8 5.6 %copy.46 = bf16[3,512,1024]{2,0,1:T(4,128)(2,1)} copy(bf16[3,512,1024]{1,2,0:T(8,128)(2,1)S(1)} %bitcast.41) | data formatting | bytes 6291456 | tf_op jit(solution)/shard_map/reshape | solution.py:344
  322.4 50.5 %all_to_all.21 = bf16[3,512,1024]{2,0,1:T(4,128)(2,1)S(1)} all-to-all(bf16[3,512,1024]{2,0,1:T(4,128)(2,1)} %copy.46), channel_id=1, replica_groups=mesh['seq'=32,'head'=4] {'head'}, dimensions={1} | all-to-all | bytes 6291456 | tf_op jit(solution)/shard_map/all_to_all | solution.py:345
  372.9 1.2 copy.47
  374.2 1.3 fusion.32
  375.5 1.6 copy.50
  377.1 1.3 copy.53
  378.4 0.7 copy.49
  379.1 1.3 copy.52
  380.4 0.0 copy-start.1
  380.4 0.7 copy.48
  381.1 1.3 copy.51
  382.4 0.0 copy-done.1
  (10 shorter events, 0.1 us)
Async XLA Ops:
  7.2 1.5 copy-start
  7.2 227.4 %reduce-scatter.2.cloned.1.call-start = ((), (), s32[]{:S(2)}) async-start(), calls=%async_computation.3 | async-start | bytes 10485760 | tf_op jit(solution)/shard_map/reduce_scatter | solution.py:337
  157.6 1.2 copy-start.3
  234.6 39.7 %copy-start.2 = (bf16[1,2,4,2,512,128]{4,5,3,2,1,0:T(8,128)(2,1)S(1)}, bf16[1,2,4,2,512,128]{4,5,3,2,1,0:T(8,128)(2,1)}, u32[]{:S(2)}) copy-start(bf16[1,2,4,2,512,128]{4,5,3,2,1,0:T(8,128)(2,1)} %reduce-scatter.2.cloned.1.call-done) | copy-start | bytes 6291460
  237.3 37.0 %collective-permute-start = (bf16[4,3,512,128]{2,3,1,0:T(8,128)(2,1)}, bf16[4,3,512,128]{2,3,1,0:T(8,128)(2,1)}, u32[]{:S(2)}, u32[]{:S(2)}) collective-permute-start(bf16[4,3,512,128]{2,3,1,0:T(8,128)(2,1)} %fusion.2), channel_id=1, source_target_pairs={{0,96},{4,100},{8,104},{12,108},{16,112},{20,116},{24,120},{28,124... | collective-permute-start | bytes 4718600 | tf_op jit(solution)/shard_map/ppermute | solution.py:341
  380.4 2.0 copy-start.1
Sparse Core Ops, SparseCore 0:
  157.8 76.7 reduce-scatter.1

commit v3 on v1

v3 whole, which is shorter than its diff:
```python
import jax
import jax.numpy as jnp
from jax import lax
from jax.experimental import pallas as pl
from jax.experimental.pallas import tpu as pltpu
from jax.sharding import PartitionSpec as P

DH = 128
BS = 64
SCALE = DH**-0.5
NT = (((1,), (1,)), ((), ()))
TN = (((0,), (0,)), ((), ()))


def dot(a, b, dims):
    return lax.dot_general(a, b, dims, preferred_element_type=jnp.float32)


MESH = pl.DeviceIdType.MESH


def index(z, x, c):
    return z * 8 + x % 4 * 2 + c


class Mover:
    def __init__(self, send, local):
        self.send, self.local = send, local
        self.sent, self.moved = [], []

    def push(self, src, dst, sem, peer):
        copy = pltpu.make_async_remote_copy(
            src_ref=src,
            dst_ref=dst,
            send_sem=self.send.at[len(self.sent)],
            recv_sem=sem,
            device_id=peer,
            device_id_type=MESH,
        )
        copy.start()
        self.sent.append(copy)

    def arrived(self, dst, sem, peer):
        pltpu.make_async_remote_copy(
            src_ref=dst,
            dst_ref=dst,
            send_sem=self.send.at[0],
            recv_sem=sem,
            device_id=peer,
            device_id_type=MESH,
        ).wait_recv()

    def move(self, src, dst):
        copy = pltpu.make_async_copy(src, dst, self.local.at[len(self.moved)])
        copy.start()
        self.moved.append(copy)
        return copy


def greet(peers):
    barrier = pltpu.get_barrier_semaphore()
    for peer in peers:
        pl.semaphore_signal(barrier, inc=1, device_id=peer, device_id_type=MESH)
    pl.semaphore_wait(barrier, len(peers))


def fetch_kernel(
    k_ref, v_ref, q_ref, g_ref, rd_ref,
    kv_out, qg_out, rdx, rdm,
    loc, oth,
    send, local, from_x, from_pair, from_mirror, from_core, from_rd,
):
    s = lax.axis_index("seq")
    z, x, c = s // 8, s // 2 % 4, s % 2
    zhi = z // 2
    mirror, pair, core = 3 - z, z + 1 - 2 * (z % 2), 1 - c
    to_mirror = {"seq": index(mirror, x, c)}
    to_pair = {"seq": index(pair, x, c)}
    to_core = {"seq": index(z, x, core)}
    along_x = [{"seq": index(z, x + d, c)} for d in range(4)]
    greet(along_x[1:] + [to_mirror, to_pair, to_core])
    mover = Mover(send, local)
    push, move = mover.push, mover.move

    def arrived(dst, sem):
        mover.arrived(dst, sem, to_core)

    ins = (k_ref, v_ref, q_ref, g_ref)
    kv = pl.ds(0, 2)
    qg = pl.ds(2, 2)

    def head(a, xx, half):
        return ins[a].at[:, pl.ds(pl.multiple_of(xx % 4 * 256 + half * DH, DH), DH)]

    def send_own(d, arrays):
        for a in arrays:
            dst = kv_out.at[s, a] if a < 2 else qg_out.at[x, a - 2]
            push(head(a, x + d, zhi), dst, from_x.at[d - 1, a, 0], along_x[d])

    def send_other(d, arrays):
        for a in arrays:
            push(head(a, x + d, 1 - zhi), oth.at[x, a], from_x.at[d - 1, a, 1], along_x[d])

    def slot_of(zz, r, cc=c):
        return kv_out.at[index(zz, x + r, cc)]

    def on_to_pair(m, r):
        slot = slot_of(mirror if m else z, r)
        push(slot, slot, from_pair.at[m, r], to_pair)
        push(slot, slot, from_core.at[m, r], to_core)

    def own_kv(r):
        for a in (0, 1):
            arrived(slot_of(z, r).at[a], from_x.at[3 - r, a, 0])
        on_to_pair(0, r)

    def other_kv(r):
        src = (x + r) % 4
        for a in (0, 1):
            arrived(oth.at[src, a], from_x.at[3 - r, a, 1])
        push(oth.at[src, kv], slot_of(z, r), from_mirror.at[0, r], to_mirror)

    def mirror_kv(r):
        arrived(slot_of(mirror, r), from_mirror.at[0, r])
        on_to_pair(1, r)

    def pair_kv(m, r):
        slot = slot_of(3 - pair if m else pair, r)
        arrived(slot, from_pair.at[m, r])
        push(slot, slot, from_core.at[2 + m, r], to_core)

    def other_qg(r):
        src = (x + r) % 4
        for a in (2, 3):
            arrived(oth.at[src, a], from_x.at[3 - r, a, 1])
        push(oth.at[src, qg], qg_out.at[4 + src], from_mirror.at[1, r], to_mirror)

    loads = [
        [move(head(a, x, zhi), loc.at[a]), move(head(a, x, 1 - zhi), oth.at[x, a])]
        for a in range(4)
    ]
    rd_load = move(rd_ref.at[x], rdx.at[x])
    send_own(1, (0, 1))
    send_own(3, (0, 1))
    send_other(1, (0, 1))
    send_other(3, (0, 1))
    for a in (0, 1):
        loads[a][0].wait()
        loads[a][1].wait()
    push(loc.at[kv], kv_out.at[s], from_pair.at[0, 0], to_pair)
    push(oth.at[x, kv], kv_out.at[s], from_mirror.at[0, 0], to_mirror)
    push(loc.at[kv], kv_out.at[s], from_core.at[0, 0], to_core)
    stores = [move(loc.at[kv], kv_out.at[s])]
    for d in (1, 2, 3):
        push(rd_ref.at[(x + d) % 4], rdx.at[x], from_rd.at[d], along_x[d])
    send_other(2, (0, 1))
    send_own(2, (0, 1))
    for d in (1, 3, 2):
        send_other(d, (2, 3))
    for d in (1, 3, 2):
        send_own(d, (2, 3))
    for a in (2, 3):
        loads[a][0].wait()
        loads[a][1].wait()
    push(oth.at[x, qg], qg_out.at[4 + x], from_mirror.at[1, 0], to_mirror)
    stores.append(move(loc.at[qg], qg_out.at[x]))
    mirror_kv(0)
    own_kv(3)
    own_kv(1)
    pair_kv(0, 0)
    other_kv(3)
    other_kv(1)
    rd_load.wait()
    for d in (1, 2, 3):
        arrived(rdx.at[(x + 4 - d) % 4], from_rd.at[d])
    push(rdx, rdm, from_rd.at[0], to_mirror)
    pair_kv(1, 0)
    mirror_kv(3)
    other_kv(2)
    mirror_kv(1)
    own_kv(2)
    pair_kv(0, 3)
    pair_kv(0, 1)
    other_qg(3)
    other_qg(1)
    mirror_kv(2)
    pair_kv(1, 3)
    other_qg(2)
    pair_kv(1, 1)
    pair_kv(0, 2)
    pair_kv(1, 2)
    for r in (3, 1, 2):
        for a in (2, 3):
            arrived(qg_out.at[(x + r) % 4, a - 2], from_x.at[3 - r, a, 0])
    for r in range(4):
        arrived(qg_out.at[4 + (x + r) % 4], from_mirror.at[1, r])
        for m, zz in enumerate((z, mirror, pair, 3 - pair)):
            arrived(slot_of(zz, r, core), from_core.at[m, r])
    arrived(rdm, from_rd.at[0])
    for copy in stores:
        copy.wait()
    for copy in mover.sent:
        copy.wait_send()


def fetch(k, v, q, g, rd):
    anywhere = pl.BlockSpec(memory_space=pl.ANY)
    vmem = pl.BlockSpec(memory_space=pltpu.VMEM)
    dma = pltpu.SemaphoreType.DMA
    return pl.pallas_call(
        fetch_kernel,
        out_shape=(
            jax.ShapeDtypeStruct((32, 2, 512, DH), jnp.bfloat16),
            jax.ShapeDtypeStruct((8, 2, 512, DH), jnp.bfloat16),
            jax.ShapeDtypeStruct((4, 8, 128), jnp.float32),
            jax.ShapeDtypeStruct((4, 8, 128), jnp.float32),
        ),
        in_specs=[anywhere] * 5,
        out_specs=(anywhere, anywhere, vmem, vmem),
        scratch_shapes=[
            pltpu.VMEM((4, 512, DH), jnp.bfloat16),
            pltpu.VMEM((4, 4, 512, DH), jnp.bfloat16),
            dma((64,)),
            dma((11,)),
            dma((3, 4, 2)),
            dma((2, 4)),
            dma((2, 4)),
            dma((4, 4)),
            dma((4,)),
        ],
        compiler_params=pltpu.CompilerParams(collective_id=0, has_side_effects=True),
    )(k, v, q, g, rd)


def give_kernel(
    dq_ref, dkv_ref, out_ref,
    part, near, far,
    send, local, from_core, from_pair, from_all,
):
    s = lax.axis_index("seq")
    y = lax.axis_index("head")
    z, x, c = s // 8, s // 2 % 4, s % 2
    zhi = z // 2
    mirror, pair, core = 3 - z, z + 1 - 2 * (z % 2), 1 - c
    to_pair = {"seq": index(pair, x, c), "head": y}
    to_core = {"seq": index(z, x, core), "head": y}
    order = (1, 3, 2, 0)

    def owner(m, r, t):
        return {"seq": index(mirror if m else z, x + r, c), "head": (y + t) % 4}

    peers = [
        owner(m, r, t) for m in (0, 1) for r in range(4) for t in range(4) if (m, r, t) != (0, 0, 0)
    ]
    greet([to_core, to_pair] + peers)
    mover = Mover(send, local)
    push, move = mover.push, mover.move
    classes = (3 - pair, pair, mirror, z)

    def spread(m, r, src, kind):
        col = pl.ds(pl.multiple_of(y * 1024 + (x * 2 + zhi) * DH, DH), DH)
        stores = []
        for t in order:
            rows = pl.ds(pl.multiple_of((y + t) % 4 * 128, 128), 128)
            if kind == 0:
                piece, dst = src.at[rows], out_ref.at[0, :, col]
            else:
                piece, dst = src.at[:, rows], out_ref.at[pl.ds(1, 2), :, col]
            if (m, r, t) == (0, 0, 0):
                stores.append(move(piece, dst))
            else:
                push(piece, dst, from_all.at[kind, m, r, t], owner(m, r, t))
        return stores

    loads = {}
    for cls in range(4):
        for r in range(4):
            at = index(classes[cls], x + r, c)
            loads[cls, r] = move(dkv_ref.at[at], part.at[cls, r])
            away = index(classes[cls], x + r, core)
            push(dkv_ref.at[away], near.at[cls, r], from_core.at[cls, r], to_core)
    kept = []
    for m in (1, 0):
        for r in order:
            kept += spread(m, r, dq_ref.at[m * 4 + (x + r) % 4], 0)

    def add(dst, terms):
        @pl.loop(0, 8)
        def _(i):
            rows = pl.ds(pl.multiple_of(i * 64, 64), 64)
            for a in range(2):
                total = terms[0][a, rows, :].astype(jnp.float32)
                for term in terms[1:]:
                    total += term[a, rows, :].astype(jnp.float32)
                dst[a, rows, :] = total.astype(jnp.bfloat16)

    for cls in (0, 1):
        for r in order:
            loads[cls, r].wait()
            mover.arrived(near.at[cls, r], from_core.at[cls, r], to_core)
            mine = part.at[cls, r]
            add(mine, (mine, near.at[cls, r]))
            push(mine, far.at[cls, r], from_pair.at[cls, r], to_pair)
    for cls in (2, 3):
        for r in order:
            loads[cls, r].wait()
            mover.arrived(near.at[cls, r], from_core.at[cls, r], to_core)
            mover.arrived(far.at[cls - 2, r], from_pair.at[cls - 2, r], to_pair)
            mine = part.at[cls, r]
            add(mine, (mine, near.at[cls, r], far.at[cls - 2, r]))
            kept += spread(3 - cls, r, mine, 1)
    for m in (0, 1):
        for r in range(4):
            for t in range(4):
                if (m, r, t) == (0, 0, 0):
                    continue
                half = 1 - zhi if m else zhi
                from_head = (x + 4 - r) % 4 * 2 + half
                col = pl.multiple_of((y + 4 - t) % 4 * 1024 + from_head * DH, DH)
                for kind in (0, 1):
                    piece = (
                        out_ref.at[0, :, pl.ds(col, DH)]
                        if kind == 0
                        else out_ref.at[pl.ds(1, 2), :, pl.ds(col, DH)]
                    )
                    mover.arrived(piece, from_all.at[kind, m, r, t], to_core)
    for copy in kept:
        copy.wait()
    for copy in mover.sent:
        copy.wait_send()


def give(dq, dkv):
    anywhere = pl.BlockSpec(memory_space=pl.ANY)
    dma = pltpu.SemaphoreType.DMA
    return pl.pallas_call(
        give_kernel,
        out_shape=jax.ShapeDtypeStruct((3, 128, 4096), jnp.bfloat16),
        in_specs=[anywhere] * 2,
        out_specs=anywhere,
        scratch_shapes=[
            pltpu.VMEM((4, 4, 2, 512, DH), jnp.bfloat16),
            pltpu.VMEM((4, 4, 2, 512, DH), jnp.bfloat16),
            pltpu.VMEM((2, 4, 2, 512, DH), jnp.bfloat16),
            dma((86,)),
            dma((18,)),
            dma((4, 4)),
            dma((2, 4)),
            dma((2, 2, 4, 4)),
        ],
        compiler_params=pltpu.CompilerParams(collective_id=1, has_side_effects=True),
    )(dq, dkv)


def attend_kernel(tab, edge, qg_ref, rd_ref, kv_ref, dq_ref, dkv_ref, acc_ref):
    acc_ref[...] = jnp.zeros_like(acc_ref)
    lane = lax.broadcasted_iota(jnp.int32, (1, 8 * BS), 1)
    eye = lax.broadcasted_iota(jnp.int32, (BS, BS), 0) == lax.broadcasted_iota(
        jnp.int32, (BS, BS), 1
    )

    def step(i, carry):
        slots = [tab[i * 8 + j] for j in range(8)]
        at = i // 8 * 16 + i % 8
        keys = jnp.concatenate([kv_ref[p] for p in slots], axis=0)
        values = jnp.concatenate([kv_ref[p + 8] for p in slots], axis=0)
        q = qg_ref[at]
        g = qg_ref[at + 8]
        state = edge[i]
        gone = ((lane < BS) & (state == 1)) | (
            (lane >= 2 * BS) & (lane < 3 * BS) & (state == 2)
        )
        bias = jnp.where(gone, -jnp.inf, 0.0)
        scores = dot(q, keys, NT) * SCALE + bias
        peak = jnp.max(scores, axis=1, keepdims=True)
        e = jnp.exp(scores - peak)
        weights = e * (1.0 / jnp.sum(e, axis=1, keepdims=True))
        rd = jnp.sum(jnp.where(eye, rd_ref[pl.ds(i, 1), :], 0.0), axis=1, keepdims=True)
        ds = weights * (dot(g, values, NT) - rd)
        wb = weights.astype(jnp.bfloat16)
        dsb = ds.astype(jnp.bfloat16)
        dq_ref[i] = (dot(dsb, keys, (((1,), (0,)), ((), ()))) * SCALE).astype(jnp.bfloat16)
        dk = dot(dsb, q, TN) * SCALE
        dv = dot(wb, g, TN)
        for j, p in enumerate(slots):
            acc_ref[p] += dk[j * BS : (j + 1) * BS]
            acc_ref[p + 8] += dv[j * BS : (j + 1) * BS]
        return carry

    lax.fori_loop(0, 64, step, 0)
    dkv_ref[...] = acc_ref[...].astype(jnp.bfloat16)


def attend(tab, edge, qg, rd, kv):
    vmem = pl.BlockSpec(memory_space=pltpu.VMEM)
    smem = pl.BlockSpec(memory_space=pltpu.SMEM)
    return pl.pallas_call(
        attend_kernel,
        out_shape=(
            jax.ShapeDtypeStruct((64, BS, DH), jnp.bfloat16),
            jax.ShapeDtypeStruct((512, BS, DH), jnp.bfloat16),
        ),
        in_specs=[smem, smem, vmem, vmem, vmem],
        out_specs=(vmem, vmem),
        scratch_shapes=[pltpu.VMEM((512, BS, DH), jnp.float32)],
        compiler_params=pltpu.CompilerParams(vmem_limit_bytes=60 * 1024 * 1024),
    )(tab, edge, qg, rd, kv)


def tables(random_blocks, global_blocks, z, x, c):
    zhi = z // 2
    mine = lax.dynamic_index_in_dim(random_blocks, x * 2 + zhi, 1, keepdims=False)
    mine = mine.reshape(4, 4, 2, 8, 3)
    mine = lax.dynamic_index_in_dim(mine, c, 2, keepdims=False)
    near = lax.dynamic_index_in_dim(mine, z, 0, keepdims=False)
    far = lax.dynamic_index_in_dim(mine, 3 - z, 0, keepdims=False)
    rand = jnp.stack([near, far]).reshape(64, 3)
    ids = jnp.arange(64, dtype=jnp.int32)
    zs = jnp.where(ids < 32, z, 3 - z)
    block = zs * 64 + ids // 8 % 4 * 16 + c * 8 + ids % 8
    window = jnp.stack([block - 1, block, block + 1], axis=1)
    window = jnp.clip(window, 0, 255)
    globs = jnp.broadcast_to(global_blocks[None], (64, 2))
    table = jnp.concatenate([window, rand, globs], axis=1)
    table = table // 8 * 16 + table % 8
    edge = jnp.where(block == 0, 1, jnp.where(block == 255, 2, 0))
    return table.reshape(512), edge


def on_device(
    queries, key_states, value_states, forward_out, grad_out, random_blocks, global_blocks
):
    s = lax.axis_index("seq")
    z, x, c = s // 8, s // 2 % 4, s % 2
    zhi = z // 2
    tab, edge = tables(random_blocks, global_blocks, z, x, c)
    row_dot = jnp.sum(
        (grad_out.astype(jnp.float32) * forward_out.astype(jnp.float32)).reshape(512, 8, DH),
        axis=2,
    )

    kv, qg, rdx, rdm = fetch(
        key_states, value_states, queries, grad_out, row_dot.T.reshape(4, 8, 128)
    )
    rd = lax.dynamic_index_in_dim(
        jnp.stack([rdx, rdm]).reshape(2, 4, 2, 512), zhi, 2, keepdims=False
    )
    dq, dkv = attend(
        tab,
        edge,
        qg.reshape(128, BS, DH),
        rd.reshape(64, BS),
        kv.reshape(512, BS, DH),
    )
    outs = give(dq.reshape(8, 512, DH), dkv.reshape(32, 2, 512, DH))
    return outs[0], outs[1], outs[2]


def solution(mesh):
    return jax.shard_map(
        on_device,
        mesh=mesh,
        in_specs=(
            P("seq", "head"),
            P("seq", "head"),
            P("seq", "head"),
            P("seq", "head"),
            P("seq", "head"),
            P(None, "head", None),
            P(),
        ),
        out_specs=(P(("seq", "head"), None), P(("seq", "head"), None), P(("seq", "head"), None)),
        check_vma=False,
    )
```

time: 460 us -> 184 us (0.40)
  waiting for transfers between devices: 214 us -> 0 us
  Pallas kernels: 49.1 us -> 171 us
  blocking collectives: 90.8 us -> 0 us
  local copies, waits for them, and re-layouts: 53.4 us -> 8.15 us
  starting transfers between devices: 17.5 us -> 0 us
  between operations: 14.3 us -> 0.85 us
  other arithmetic: 16.3 us -> 3.78 us
    pallas_call x0 -> x2, Pallas kernels: none -> 122 us  [the longest x1 64.3 us: give(): pl.pallas_call(give_kernel, out_shape=jax.ShapeDtypeStruct((3, 128, 4096)...]
    all_to_all x2 -> x0, blocking collectives: 90.8 us -> none  [the longest x1 50.5 us: on_device(): outs = lax.all_to_all(rows, 'head', split_axis=1, concat_axis=2, tiled=True)]
    reduce_scatter x1 -> x0, waiting for transfers between devices: 78.2 us -> none  [on_device(): lax.psum_scatter(dkv.reshape(4, 2, 4, 2, 512, DH), 'seq', axis_index_grou...]
    ppermute x4 -> x0, waiting for transfers between devices: 73 us -> none  [the longest x3 38.3 us: to_head(): return jnp.stack([own, lax.ppermute(other, 'seq', MIRROR)])]
    all_to_all x3 -> x0, waiting for transfers between devices: 43.1 us -> none  [over_x(): lax.all_to_all(a, 'seq', 0, 0, axis_index_groups=X_GROUPS, tiled=True)]
    all_gather x1 -> x0, waiting for transfers between devices: 19.8 us -> none  [on_device(): kv = lax.all_gather(kv, 'seq', axis_index_groups=HEAD_GROUPS)]
    reshape x4 -> x1, local copies, waits for them, and re-layouts: 20 us -> 0.62 us  [on_device(): row_dot.T.reshape(4, 8, 128)]
    unnamed x28 -> x3, local copies, waits for them, and re-layouts: 14 us -> 0.48 us
  transfers between devices with their start and end apart: 9 -> 0, of which waited for: 8 -> 0; matrix products, arithmetic and copies ran while one was open for 4% -> 0% of each run, Pallas kernels for 0% -> 0%
where the time goes in v3:
time: 184 us
  Pallas kernels  171 us (93%)
  local copies, waits for them, and re-layouts  8.15 us (4%)
  other arithmetic  3.78 us (2%)
    pallas_call x1, Pallas kernels, give(): pl.pallas_call(give_kernel, out_shape=jax.ShapeDtypeStruct((3, 128, 4096)...  64.3 us
    pallas_call x1, Pallas kernels, fetch(): pl.pallas_call(fetch_kernel, out_shape=(jax.ShapeDtypeStruct((32, 2, 512,...  57.8 us
    pallas_call x1, Pallas kernels, attend(): pl.pallas_call(attend_kernel, out_shape=(jax.ShapeDtypeStruct((64, BS, DH...  49 us

profile of v3, /device:TPU:33, one launch (start us, length us, event | category | flops | bytes accessed | tf_op | source)
XLA Modules:
  0.0 184.0 jit_solution(198720894067842844)
XLA Ops:
  0.6 0.0 copy-start
  0.7 0.7 pad.4.clone
  1.5 0.5 compare_select_fusion.5.edge
  2.0 0.0 copy-done
  2.1 0.1 reshape.159
  2.3 0.1 reshape.160
  2.4 0.1 add_add_fusion
  2.4 0.1 copy.17
  2.5 0.1 concatenate.7
  2.6 0.6 fusion.2.tab
  3.2 1.9 %multiply_bitcast_fusion = f32[64,8,8,128]{3,1,2,0:T(8,128)S(1)} fusion(bf16[512,1024]{1,0:T(8,128)(2,1)} %param.10, bf16[512,1024]{1,0:T(8,128)(2,1)} %g_ref.1), kind=kLoop, calls=%fused_computation | loop fusion | flops 1572864 | bytes 4194304
  5.1 0.5 copy.21
  5.6 0.6 reduce_sum.9
  6.2 0.1 copy.18
  6.3 0.6 reshape.162.rd_ref
  7.0 57.8 %shard_map.94 = (bf16[32,2,512,128]{3,2,1,0:T(8,128)(2,1)}, bf16[8,2,512,128]{3,2,1,0:T(8,128)(2,1)}, f32[4,8,128]{2,1,0:T(8,128)}, f32[4,8,128]{2,1,0:T(8,128)}) custom-call(bf16[512,1024]{1,0:T(8,128)(2,1)} %k_ref.1, bf16[512,1024]{1,0:T(8,128)(2,1)} %v_ref.1, bf16[512,1024]{1,0:T(8,128)(2,1)} %q_ref.1, bf16[512,1024]{1,0:T(8,128)(2,1)} %g_ref.1, ...), custom_call_target="tpu_custom_call" | custom-call | tf_op jit(solution)/shard_map/pallas_call | solution.py:210
  64.8 0.7 stack.22
  65.5 0.7 stack.23
  66.3 0.7 reshape.164.rd_ref
  67.0 49.0 %shard_map.95 = (bf16[64,64,128]{2,1,0:T(8,128)(2,1)}, bf16[512,64,128]{2,1,0:T(8,128)(2,1)}) custom-call(s32[512]{0:T(512)} %fusion.2.tab, s32[64]{0:T(128)} %compare_select_fusion.5.edge, bf16[128,64,128]{2,1,0:T(8,128)(2,1)} %bitcast.25, f32[64,64]{1,0:T(8,128)} %reshape.164.rd_ref, bf16[512,64,128]{2,1,0:T(8,128)(2,1)} %bitcast.24), custom_call_target="tpu_custom_call" | custom-call | tf_op jit(solution)/shard_map/pallas_call | solution.py:397
  116.0 64.3 %shard_map.96 = bf16[3,128,4096]{2,1,0:T(8,128)(2,1)} custom-call(bf16[8,512,128]{2,1,0:T(8,128)(2,1)} %bitcast.26, bf16[32,2,512,128]{3,2,1,0:T(8,128)(2,1)} %bitcast.22), custom_call_target="tpu_custom_call" | custom-call | tf_op jit(solution)/shard_map/pallas_call | solution.py:336
  180.3 3.6 %slice_bitcast_fusion = (bf16[128,4096]{1,0:T(8,128)(2,1)}, bf16[128,4096]{1,0:T(8,128)(2,1)}, bf16[128,4096]{1,0:T(8,128)(2,1)}) fusion(bf16[3,128,4096]{2,1,0:T(8,128)(2,1)} %shard_map.96), kind=kLoop, calls=%fused_computation.1 | loop fusion | bytes 6291456 | tf_op jit(solution)/shard_map/squeeze | solution.py:456
  (10 shorter events, 0.1 us)
Async XLA Ops:
  0.6 1.4 copy-start

commit v4 on v3

--- a/solution.py
+++ b/solution.py
@@ -8,8 +8,11 @@
 DH = 128
 BS = 64
 SCALE = DH**-0.5
+SCALE_LOG2E = SCALE * 1.4426950408889634
+ATTEND_VMEM = 60 * 1024 * 1024
 NT = (((1,), (1,)), ((), ()))
 TN = (((0,), (0,)), ((), ()))
+NN = (((1,), (0,)), ((), ()))
 
 
 def dot(a, b, dims):
@@ -65,9 +68,9 @@
 
 
 def fetch_kernel(
-    k_ref, v_ref, q_ref, g_ref, rd_ref,
-    kv_out, qg_out, rdx, rdm,
-    loc, oth,
+    k_ref, v_ref, q_ref, g_ref, o_ref,
+    kv_out, qg_out, rd_out,
+    loc, oth, rd_mine, g_all, o_all,
     send, local, from_x, from_pair, from_mirror, from_core, from_rd,
 ):
     s = lax.axis_index("seq")
@@ -139,7 +142,7 @@
         [move(head(a, x, zhi), loc.at[a]), move(head(a, x, 1 - zhi), oth.at[x, a])]
         for a in range(4)
     ]
-    rd_load = move(rd_ref.at[x], rdx.at[x])
+    dots = [move(g_ref, g_all), move(o_ref, o_all)]
     send_own(1, (0, 1))
     send_own(3, (0, 1))
     send_other(1, (0, 1))
@@ -151,8 +154,6 @@
     push(oth.at[x, kv], kv_out.at[s], from_mirror.at[0, 0], to_mirror)
     push(loc.at[kv], kv_out.at[s], from_core.at[0, 0], to_core)
     stores = [move(loc.at[kv], kv_out.at[s])]
-    for d in (1, 2, 3):
-        push(rd_ref.at[(x + d) % 4], rdx.at[x], from_rd.at[d], along_x[d])
     send_other(2, (0, 1))
     send_own(2, (0, 1))
     for d in (1, 3, 2):
@@ -164,21 +165,36 @@
         loads[a][1].wait()
     push(oth.at[x, qg], qg_out.at[4 + x], from_mirror.at[1, 0], to_mirror)
     stores.append(move(loc.at[qg], qg_out.at[x]))
+    for load in dots:
+        load.wait()
+
+    @pl.loop(0, 4)
+    def _(i):
+        rows = pl.ds(pl.multiple_of(i * 128, 128), 128)
+        for h in range(8):
+            cols = slice(h * DH, (h + 1) * DH)
+            terms = g_all[rows, cols].astype(jnp.float32) * o_all[rows, cols].astype(jnp.float32)
+            rd_mine[h // 2, pl.ds(h % 2 * 4 + i, 1), :] = jnp.sum(terms.T, axis=0, keepdims=True)
+
     mirror_kv(0)
     own_kv(3)
     own_kv(1)
     pair_kv(0, 0)
+    rd_load = move(rd_mine.at[x], rd_out.at[x])
+    for d in (1, 2, 3):
+        push(rd_mine.at[(x + d) % 4], rd_out.at[x], from_rd.at[d], along_x[d])
     other_kv(3)
     other_kv(1)
-    rd_load.wait()
-    for d in (1, 2, 3):
-        arrived(rdx.at[(x + 4 - d) % 4], from_rd.at[d])
-    push(rdx, rdm, from_rd.at[0], to_mirror)
     pair_kv(1, 0)
     mirror_kv(3)
     other_kv(2)
     mirror_kv(1)
     own_kv(2)
+    rd_load.wait()
+    for d in (1, 2, 3):
+        arrived(rd_out.at[(x + 4 - d) % 4], from_rd.at[d])
+    near, far = pl.ds(0, 4), pl.ds(4, 4)
+    push(rd_out.at[near], rd_out.at[far], from_rd.at[0], to_mirror)
     pair_kv(0, 3)
     pair_kv(0, 1)
     other_qg(3)
@@ -196,14 +212,14 @@
         arrived(qg_out.at[4 + (x + r) % 4], from_mirror.at[1, r])
         for m, zz in enumerate((z, mirror, pair, 3 - pair)):
             arrived(slot_of(zz, r, core), from_core.at[m, r])
-    arrived(rdm, from_rd.at[0])
+    arrived(rd_out.at[far], from_rd.at[0])
     for copy in stores:
         copy.wait()
     for copy in mover.sent:
         copy.wait_send()
 
 
-def fetch(k, v, q, g, rd):
+def fetch(k, v, q, g, o):
     anywhere = pl.BlockSpec(memory_space=pl.ANY)
     vmem = pl.BlockSpec(memory_space=pltpu.VMEM)
     dma = pltpu.SemaphoreType.DMA
@@ -212,16 +228,18 @@
         out_shape=(
             jax.ShapeDtypeStruct((32, 2, 512, DH), jnp.bfloat16),
             jax.ShapeDtypeStruct((8, 2, 512, DH), jnp.bfloat16),
-            jax.ShapeDtypeStruct((4, 8, 128), jnp.float32),
-            jax.ShapeDtypeStruct((4, 8, 128), jnp.float32),
+            jax.ShapeDtypeStruct((8, 8, 128), jnp.float32),
         ),
         in_specs=[anywhere] * 5,
-        out_specs=(anywhere, anywhere, vmem, vmem),
+        out_specs=(anywhere, anywhere, vmem),
         scratch_shapes=[
             pltpu.VMEM((4, 512, DH), jnp.bfloat16),
             pltpu.VMEM((4, 4, 512, DH), jnp.bfloat16),
+            pltpu.VMEM((4, 8, 128), jnp.float32),
+            pltpu.VMEM((512, 1024), jnp.bfloat16),
+            pltpu.VMEM((512, 1024), jnp.bfloat16),
             dma((64,)),
-            dma((11,)),
+            dma((13,)),
             dma((3, 4, 2)),
             dma((2, 4)),
             dma((2, 4)),
@@ -229,7 +247,7 @@
             dma((4,)),
         ],
         compiler_params=pltpu.CompilerParams(collective_id=0, has_side_effects=True),
-    )(k, v, q, g, rd)
+    )(k, v, q, g, o)
 
 
 def give_kernel(
@@ -274,7 +292,7 @@
 
     loads = {}
     for cls in range(4):
-        for r in range(4):
+        for r in order:
             at = index(classes[cls], x + r, c)
             loads[cls, r] = move(dkv_ref.at[at], part.at[cls, r])
             away = index(classes[cls], x + r, core)
@@ -352,58 +370,137 @@
     )(dq, dkv)
 
 
-def attend_kernel(tab, edge, qg_ref, rd_ref, kv_ref, dq_ref, dkv_ref, acc_ref):
-    acc_ref[...] = jnp.zeros_like(acc_ref)
-    lane = lax.broadcasted_iota(jnp.int32, (1, 8 * BS), 1)
-    eye = lax.broadcasted_iota(jnp.int32, (BS, BS), 0) == lax.broadcasted_iota(
-        jnp.int32, (BS, BS), 1
-    )
-
-    def step(i, carry):
-        slots = [tab[i * 8 + j] for j in range(8)]
-        at = i // 8 * 16 + i % 8
-        keys = jnp.concatenate([kv_ref[p] for p in slots], axis=0)
-        values = jnp.concatenate([kv_ref[p + 8] for p in slots], axis=0)
-        q = qg_ref[at]
-        g = qg_ref[at + 8]
-        state = edge[i]
-        gone = ((lane < BS) & (state == 1)) | (
-            (lane >= 2 * BS) & (lane < 3 * BS) & (state == 2)
+def attend_kernel(
+    tab, edge, qg_hbm, rd_ref, kv_hbm, dq_ref, dkv_hbm,
+    qg_ref, kv_ref, acc_ref, s0, s1, w0, w1, d0, d1, p0, p1, arrive, leave,
+):
+    loads = [
+        pltpu.make_async_copy(
+            kv_hbm.at[pl.ds(i * 128, 128)], kv_ref.at[pl.ds(i * 128, 128)], arrive.at[i]
         )
-        bias = jnp.where(gone, -jnp.inf, 0.0)
-        scores = dot(q, keys, NT) * SCALE + bias
-        peak = jnp.max(scores, axis=1, keepdims=True)
-        e = jnp.exp(scores - peak)
-        weights = e * (1.0 / jnp.sum(e, axis=1, keepdims=True))
-        rd = jnp.sum(jnp.where(eye, rd_ref[pl.ds(i, 1), :], 0.0), axis=1, keepdims=True)
-        ds = weights * (dot(g, values, NT) - rd)
-        wb = weights.astype(jnp.bfloat16)
-        dsb = ds.astype(jnp.bfloat16)
-        dq_ref[i] = (dot(dsb, keys, (((1,), (0,)), ((), ()))) * SCALE).astype(jnp.bfloat16)
-        dk = dot(dsb, q, TN) * SCALE
-        dv = dot(wb, g, TN)
-        for j, p in enumerate(slots):
-            acc_ref[p] += dk[j * BS : (j + 1) * BS]
-            acc_ref[p + 8] += dv[j * BS : (j + 1) * BS]
-        return carry
-
-    lax.fori_loop(0, 64, step, 0)
-    dkv_ref[...] = acc_ref[...].astype(jnp.bfloat16)
+        for i in range(4)
+    ]
+    loads.append(pltpu.make_async_copy(qg_hbm, qg_ref, arrive.at[4]))
+    for load in loads:
+        load.start()
+
+    @pl.loop(0, 32)
+    def _(i):
+        acc_ref[pl.ds(i * 16, 16)] = jnp.zeros((16, BS, DH), jnp.float32)
+
+    for load in loads:
+        load.wait()
+    first = lax.broadcasted_iota(jnp.int32, (1, 2 * BS), 1) < BS
+    half = edge[64] * 4
+
+    def slots_of(p):
+        return [tab[p * 16 + j] for j in range(16)]
+
+    def base_of(p):
+        return p // 4 * 16 + p % 4 * 2
+
+    def pair_rows(base):
+        a, b = qg_ref[base], qg_ref[base + 1]
+        zero = jnp.zeros_like(a)
+        return jnp.concatenate(
+            [jnp.concatenate([a, zero], axis=1), jnp.concatenate([zero, b], axis=1)], axis=0
+        )
+
+    def pair_keys(slots, offset):
+        return jnp.concatenate(
+            [
+                jnp.concatenate([kv_ref[slots[j] + offset], kv_ref[slots[8 + j] + offset]], axis=1)
+                for j in range(8)
+            ],
+            axis=0,
+        )
+
+    def score(p, s_ref, w_ref):
+        slots, base = slots_of(p), base_of(p)
+        s_ref[...] = dot(pair_keys(slots, 0), pair_rows(base), NT)
+        w_ref[...] = dot(pair_keys(slots, 8), pair_rows(base + 8), NT)
+
+    def soften(p, s_ref, w_ref, d_ref, p_ref):
+        state = jnp.where(first, edge[2 * p], edge[2 * p + 1])
+        low = jnp.where(state == 1, -jnp.inf, 0.0)
+        high = jnp.where(state == 2, -jnp.inf, 0.0)
+        s = s_ref[...] * SCALE_LOG2E
+        s = jnp.concatenate(
+            [s[:BS] + low, s[BS : 2 * BS], s[2 * BS : 3 * BS] + high, s[3 * BS :]], axis=0
+        )
+        e = jnp.exp2(s - jnp.max(s, axis=0, keepdims=True))
+        weights = e * (1.0 / jnp.sum(e, axis=0, keepdims=True))
+        p_ref[...] = weights.astype(jnp.bfloat16)
+        rd = rd_ref[p // 4, pl.ds(half + p % 4, 1), :]
+        d_ref[...] = (weights * (w_ref[...] - rd)).astype(jnp.bfloat16)
+
+    def spread(p, d_ref, p_ref):
+        slots, base = slots_of(p), base_of(p)
+        d = d_ref[...]
+        dq = dot(d, pair_keys(slots, 0), TN) * SCALE
+        dq_ref[2 * p] = dq[:BS, :DH].astype(jnp.bfloat16)
+        dq_ref[2 * p + 1] = dq[BS:, DH:].astype(jnp.bfloat16)
+        dk = dot(d, pair_rows(base), NN)
+        dv = dot(p_ref[...], pair_rows(base + 8), NN)
+        for j in range(16):
+            side, row = j // 8 * DH, j % 8 * BS
+            acc_ref[slots[j]] += dk[row : row + BS, side : side + DH]
+            acc_ref[slots[j] + 8] += dv[row : row + BS, side : side + DH]
+
+    score(0, s0, w0)
+    soften(0, s0, w0, d0, p0)
+    score(1, s1, w1)
+
+    @pl.loop(1, 16)
+    def _(t):
+        a = 2 * t
+        spread(a - 2, d0, p0)
+        soften(a - 1, s1, w1, d1, p1)
+        score(a, s0, w0)
+        spread(a - 1, d1, p1)
+        soften(a, s0, w0, d0, p0)
+        score(a + 1, s1, w1)
+
+    soften(31, s1, w1, d1, p1)
+    spread(30, d0, p0)
+    spread(31, d1, p1)
+    stores = []
+    for i in range(8):
+
+        @pl.loop(0, 4)
+        def _(t):
+            slot = pl.multiple_of(i * 64 + t * 16, 16)
+            kv_ref[pl.ds(slot, 8)] = (acc_ref[pl.ds(slot, 8)] * SCALE).astype(jnp.bfloat16)
+            kv_ref[pl.ds(slot + 8, 8)] = acc_ref[pl.ds(slot + 8, 8)].astype(jnp.bfloat16)
+
+        part = pl.ds(i * 64, 64)
+        stores.append(pltpu.make_async_copy(kv_ref.at[part], dkv_hbm.at[part], leave.at[i]))
+        stores[-1].start()
+    for store in stores:
+        store.wait()
 
 
 def attend(tab, edge, qg, rd, kv):
     vmem = pl.BlockSpec(memory_space=pltpu.VMEM)
     smem = pl.BlockSpec(memory_space=pltpu.SMEM)
+    anywhere = pl.BlockSpec(memory_space=pl.ANY)
     return pl.pallas_call(
         attend_kernel,
         out_shape=(
             jax.ShapeDtypeStruct((64, BS, DH), jnp.bfloat16),
             jax.ShapeDtypeStruct((512, BS, DH), jnp.bfloat16),
         ),
-        in_specs=[smem, smem, vmem, vmem, vmem],
-        out_specs=(vmem, vmem),
-        scratch_shapes=[pltpu.VMEM((512, BS, DH), jnp.float32)],
-        compiler_params=pltpu.CompilerParams(vmem_limit_bytes=60 * 1024 * 1024),
+        in_specs=[smem, smem, anywhere, vmem, anywhere],
+        out_specs=(vmem, anywhere),
+        scratch_shapes=[
+            pltpu.VMEM((128, BS, DH), jnp.bfloat16),
+            pltpu.VMEM((512, BS, DH), jnp.bfloat16),
+            pltpu.VMEM((512, BS, DH), jnp.float32),
+        ]
+        + [pltpu.VMEM((8 * BS, 2 * BS), jnp.float32)] * 4
+        + [pltpu.VMEM((8 * BS, 2 * BS), jnp.bfloat16)] * 4
+        + [pltpu.SemaphoreType.DMA((5,)), pltpu.SemaphoreType.DMA((8,))],
+        compiler_params=pltpu.CompilerParams(vmem_limit_bytes=ATTEND_VMEM),
     )(tab, edge, qg, rd, kv)
 
 
@@ -424,6 +521,7 @@
     table = jnp.concatenate([window, rand, globs], axis=1)
     table = table // 8 * 16 + table % 8
     edge = jnp.where(block == 0, 1, jnp.where(block == 255, 2, 0))
+    edge = jnp.concatenate([edge, zhi[None].astype(edge.dtype)])
     return table.reshape(512), edge
 
 
@@ -434,22 +532,12 @@
     z, x, c = s // 8, s // 2 % 4, s % 2
     zhi = z // 2
     tab, edge = tables(random_blocks, global_blocks, z, x, c)
-    row_dot = jnp.sum(
-        (grad_out.astype(jnp.float32) * forward_out.astype(jnp.float32)).reshape(512, 8, DH),
-        axis=2,
-    )
-
-    kv, qg, rdx, rdm = fetch(
-        key_states, value_states, queries, grad_out, row_dot.T.reshape(4, 8, 128)
-    )
-    rd = lax.dynamic_index_in_dim(
-        jnp.stack([rdx, rdm]).reshape(2, 4, 2, 512), zhi, 2, keepdims=False
-    )
+    kv, qg, rd = fetch(key_states, value_states, queries, grad_out, forward_out)
     dq, dkv = attend(
         tab,
         edge,
         qg.reshape(128, BS, DH),
-        rd.reshape(64, BS),
+        rd,
         kv.reshape(512, BS, DH),
     )
     outs = give(dq.reshape(8, 512, DH), dkv.reshape(32, 2, 512, DH))

time: 184 us -> 165 us (0.90)
  Pallas kernels: 171 us -> 158 us
  local copies, waits for them, and re-layouts: 8.15 us -> 4.8 us
  other arithmetic: 3.78 us -> 1.31 us
    pallas_call x1, Pallas kernels: 49 us -> 23.2 us  [attend(): pl.pallas_call(attend_kernel, out_shape=(jax.ShapeDtypeStruct((64, BS, DH...]
    pallas_call x1, Pallas kernels: 57.8 us -> 70.2 us  [fetch(): pl.pallas_call(fetch_kernel, out_shape=(jax.ShapeDtypeStruct((32, 2, 512,...]
    unnamed x1 -> x0, other arithmetic: 1.92 us -> none
where the time goes in v4:
time: 165 us
  Pallas kernels  158 us (96%)
  local copies, waits for them, and re-layouts  4.8 us (3%)
    pallas_call x1, Pallas kernels, fetch(): pl.pallas_call(fetch_kernel, out_shape=(jax.ShapeDtypeStruct((32, 2, 512,...  70.2 us
    pallas_call x1, Pallas kernels, give(): pl.pallas_call(give_kernel, out_shape=jax.ShapeDtypeStruct((3, 128, 4096)...  64.4 us
    pallas_call x1, Pallas kernels, attend(): pl.pallas_call(attend_kernel, out_shape=(jax.ShapeDtypeStruct((64, BS, DH...  23.2 us
    squeeze x1, local copies, waits for them, and re-layouts, on_device(): return (outs[0], outs[1], outs[2])  3.61 us

profile of v4, /device:TPU:33, one launch (start us, length us, event | category | flops | bytes accessed | tf_op | source)
XLA Modules:
  0.0 164.8 jit_solution(13071161924104495278)
XLA Ops:
  0.6 0.0 copy-start
  0.7 0.7 pad.4.clone
  1.5 0.6 pad_add_fusion.1.edge
  2.1 0.0 copy-done
  2.2 0.1 reshape.144
  2.3 0.1 reshape.145
  2.4 0.1 add_add_fusion
  2.5 0.1 copy.11
  2.6 0.1 concatenate.9
  2.7 0.6 fusion.1.tab
  3.3 70.2 %shard_map.94 = (bf16[32,2,512,128]{3,2,1,0:T(8,128)(2,1)}, bf16[8,2,512,128]{3,2,1,0:T(8,128)(2,1)}, f32[8,8,128]{2,1,0:T(8,128)}) custom-call(bf16[512,1024]{1,0:T(8,128)(2,1)} %k_ref.1, bf16[512,1024]{1,0:T(8,128)(2,1)} %v_ref.1, bf16[512,1024]{1,0:T(8,128)(2,1)} %q_ref.1, bf16[512,1024]{1,0:T(8,128)(2,1)} %g_ref.1, bf16[512,1024]{1,0:T(8,128)(2,1)} %o_ref.1), custom_call_target="tpu_custom_call" | custom-call | tf_op jit(solution)/shard_map/pallas_call | solution.py:226
  73.5 23.2 %shard_map.95 = (bf16[64,64,128]{2,1,0:T(8,128)(2,1)}, bf16[512,64,128]{2,1,0:T(8,128)(2,1)}) custom-call(s32[512]{0:T(512)} %fusion.1.tab, s32[65]{0:T(128)} %pad_add_fusion.1.edge, bf16[128,64,128]{2,1,0:T(8,128)(2,1)} %bitcast.19, f32[8,8,128]{2,1,0:T(8,128)} %get-tuple-element.9.rd_ref, bf16[512,64,128]{2,1,0:T(8,128)(2,1)} %bitcast.18), custom_call_target="tpu_custom_call" | custom-call | tf_op jit(solution)/shard_map/pallas_call | solution.py:487
  96.8 64.4 %shard_map.96 = bf16[3,128,4096]{2,1,0:T(8,128)(2,1)} custom-call(bf16[8,512,128]{2,1,0:T(8,128)(2,1)} %bitcast.20, bf16[32,2,512,128]{3,2,1,0:T(8,128)(2,1)} %bitcast.17), custom_call_target="tpu_custom_call" | custom-call | tf_op jit(solution)/shard_map/pallas_call | solution.py:354
  161.2 3.6 %slice_bitcast_fusion = (bf16[128,4096]{1,0:T(8,128)(2,1)}, bf16[128,4096]{1,0:T(8,128)(2,1)}, bf16[128,4096]{1,0:T(8,128)(2,1)}) fusion(bf16[3,128,4096]{2,1,0:T(8,128)(2,1)} %shard_map.96), kind=kLoop, calls=%fused_computation | loop fusion | bytes 6291456 | tf_op jit(solution)/shard_map/squeeze | solution.py:544
  (8 shorter events, 0.1 us)
Async XLA Ops:
  0.6 1.5 copy-start

commit v5 on v4

v5 whole, which is shorter than its diff:
```python
import jax
import jax.numpy as jnp
from jax import lax
from jax.experimental import pallas as pl
from jax.experimental.pallas import tpu as pltpu
from jax.sharding import PartitionSpec as P

DH = 128
BS = 64
SCALE = DH**-0.5
SCALE_LOG2E = SCALE * 1.4426950408889634
ATTEND_VMEM = 24 * 1024 * 1024
FETCH_VMEM = 10 * 1024 * 1024
GIVE_VMEM = 16 * 1024 * 1024
NT = (((1,), (1,)), ((), ()))
TN = (((0,), (0,)), ((), ()))
NN = (((1,), (0,)), ((), ()))


def dot(a, b, dims):
    return lax.dot_general(a, b, dims, preferred_element_type=jnp.float32)


MESH = pl.DeviceIdType.MESH


def index(z, x, c):
    return z * 8 + x % 4 * 2 + c


class Mover:
    def __init__(self, send, local):
        self.send, self.local = send, local
        self.sent, self.moved = [], []

    def push(self, src, dst, sem, peer):
        copy = pltpu.make_async_remote_copy(
            src_ref=src,
            dst_ref=dst,
            send_sem=self.send.at[len(self.sent)],
            recv_sem=sem,
            device_id=peer,
            device_id_type=MESH,
        )
        copy.start()
        self.sent.append(copy)

    def arrived(self, dst, sem, peer):
        pltpu.make_async_remote_copy(
            src_ref=dst,
            dst_ref=dst,
            send_sem=self.send.at[0],
            recv_sem=sem,
            device_id=peer,
            device_id_type=MESH,
        ).wait_recv()

    def move(self, src, dst):
        copy = pltpu.make_async_copy(src, dst, self.local.at[len(self.moved)])
        copy.start()
        self.moved.append(copy)
        return copy


def greet(peers):
    barrier = pltpu.get_barrier_semaphore()
    for peer in peers:
        pl.semaphore_signal(barrier, inc=1, device_id=peer, device_id_type=MESH)
    pl.semaphore_wait(barrier, len(peers))


def fetch_kernel(
    k_ref, v_ref, q_ref, g_ref, o_ref,
    kv_out, qg_out, rd_out,
    oth, rd_mine, g_all, o_all,
    send, local, from_x, from_pair, from_mirror, from_core, from_rd,
):
    s = lax.axis_index("seq")
    z, x, c = s // 8, s // 2 % 4, s % 2
    zhi = z // 2
    mirror, pair, core = 3 - z, z + 1 - 2 * (z % 2), 1 - c
    to_mirror = {"seq": index(mirror, x, c)}
    to_pair = {"seq": index(pair, x, c)}
    to_core = {"seq": index(z, x, core)}
    along_x = [{"seq": index(z, x + d, c)} for d in range(4)]
    mover = Mover(send, local)
    push, move = mover.push, mover.move

    def arrived(dst, sem):
        mover.arrived(dst, sem, to_core)

    ins = (k_ref, v_ref, q_ref, g_ref)

    def head(a, xx, half):
        return ins[a].at[:, pl.ds(pl.multiple_of(xx % 4 * 256 + half * DH, DH), DH)]

    def send_own(d, a):
        dst = kv_out.at[s, a] if a < 2 else qg_out.at[x, a - 2]
        push(head(a, x + d, zhi), dst, from_x.at[d - 1, a, 0], along_x[d])

    def send_other(d, a):
        push(head(a, x + d, 1 - zhi), oth.at[x, a], from_x.at[d - 1, a, 1], along_x[d])

    def at(zz, r, a, cc=c):
        return kv_out.at[index(zz, x + r, cc), a]

    def forward(src, dst, m, r, a):
        push(src, dst, from_pair.at[m, r, a], to_pair)
        push(src, dst, from_core.at[m, r, a], to_core)

    def own(r, a):
        piece = at(z, r, a)
        arrived(piece, from_x.at[3 - r, a, 0])
        forward(piece, piece, 0, r, a)

    def other(r, a):
        src = (x + r) % 4
        arrived(oth.at[src, a], from_x.at[3 - r, a, 1])
        dst = at(z, r, a) if a < 2 else qg_out.at[4 + src, a - 2]
        push(oth.at[src, a], dst, from_mirror.at[r, a], to_mirror)

    def mirrored(r, a):
        piece = at(mirror, r, a)
        arrived(piece, from_mirror.at[r, a])
        forward(piece, piece, 1, r, a)

    def paired(m, r, a):
        piece = at(3 - pair if m else pair, r, a)
        arrived(piece, from_pair.at[m, r, a])
        push(piece, piece, from_core.at[2 + m, r, a], to_core)

    dots = [move(g_ref, g_all), move(o_ref, o_all)]
    greet(along_x[1:] + [to_mirror, to_pair, to_core])
    for a in (0, 1):
        push(head(a, x, zhi), at(z, 0, a), from_pair.at[0, 0, a], to_pair)
        push(head(a, x, 1 - zhi), at(z, 0, a), from_mirror.at[0, a], to_mirror)
        send_own(1, a)
        send_own(3, a)
    for a in (0, 1):
        send_other(1, a)
        send_other(3, a)
        push(head(a, x, zhi), at(z, 0, a), from_core.at[0, 0, a], to_core)
    stores = [move(head(a, x, zhi), at(z, 0, a)) for a in (0, 1)]
    stores += [move(head(a, x, zhi), qg_out.at[x, a - 2]) for a in (2, 3)]
    for a in (0, 1):
        send_other(2, a)
    for a in (0, 1):
        send_own(2, a)
    for a in (2, 3):
        push(head(a, x, 1 - zhi), qg_out.at[4 + x, a - 2], from_mirror.at[0, a], to_mirror)
    for load in dots:
        load.wait()
    ones = jnp.ones((16, 2 * DH), jnp.bfloat16)
    for h in range(8):
        cols = slice(h * DH, (h + 1) * DH)
        terms = g_all[:, cols].astype(jnp.float32) * o_all[:, cols].astype(jnp.float32)
        high = terms.astype(jnp.bfloat16)
        low = (terms - high.astype(jnp.float32)).astype(jnp.bfloat16)
        sums = dot(ones, jnp.concatenate([high, low], axis=1), NT)
        for t in range(4):
            rd_mine[h // 2, h % 2 * 4 + t : h % 2 * 4 + t + 1, :] = sums[
                0:1, t * 128 : (t + 1) * 128
            ]
    own(3, 0)
    own(1, 0)
    mirrored(0, 0)
    own(3, 1)
    own(1, 1)
    mirrored(0, 1)
    rd_load = move(rd_mine.at[x], rd_out.at[x])
    for d in (1, 2, 3):
        push(rd_mine.at[(x + d) % 4], rd_out.at[x], from_rd.at[d], along_x[d])
    for d in (1, 3, 2):
        for a in (2, 3):
            send_other(d, a)
    for d in (1, 3, 2):
        for a in (2, 3):
            send_own(d, a)
    other(3, 0)
    other(1, 0)
    paired(0, 0, 0)
    paired(0, 0, 1)
    other(3, 1)
    other(1, 1)
    paired(0, 3, 0)
    paired(0, 1, 0)
    mirrored(3, 0)
    other(2, 0)
    mirrored(1, 0)
    other(2, 1)
    paired(1, 0, 0)
    paired(0, 3, 1)
    mirrored(3, 1)
    paired(0, 1, 1)
    own(2, 0)
    mirrored(1, 1)
    own(2, 1)
    mirrored(2, 0)
    paired(1, 0, 1)
    other(3, 2)
    other(1, 2)
    mirrored(2, 1)
    other(3, 3)
    other(1, 3)
    rd_load.wait()
    for d in (1, 2, 3):
        arrived(rd_out.at[(x + 4 - d) % 4], from_rd.at[d])
    near, far = pl.ds(0, 4), pl.ds(4, 4)
    push(rd_out.at[near], rd_out.at[far], from_rd.at[0], to_mirror)
    paired(1, 3, 0)
    paired(1, 1, 0)
    other(2, 2)
    other(2, 3)
    paired(1, 3, 1)
    paired(0, 2, 0)
    paired(1, 1, 1)
    paired(0, 2, 1)
    paired(1, 2, 0)
    paired(1, 2, 1)
    for r in (3, 1, 2):
        for a in (2, 3):
            arrived(qg_out.at[(x + r) % 4, a - 2], from_x.at[3 - r, a, 0])
    for r in range(4):
        for a in (0, 1):
            arrived(qg_out.at[4 + (x + r) % 4, a], from_mirror.at[r, 2 + a])
            for m, zz in enumerate((z, mirror, pair, 3 - pair)):
                arrived(at(zz, r, a, core), from_core.at[m, r, a])
    arrived(rd_out.at[far], from_rd.at[0])
    for copy in stores:
        copy.wait()
    for copy in mover.sent:
        copy.wait_send()


def fetch(k, v, q, g, o):
    anywhere = pl.BlockSpec(memory_space=pl.ANY)
    vmem = pl.BlockSpec(memory_space=pltpu.VMEM)
    dma = pltpu.SemaphoreType.DMA
    return pl.pallas_call(
        fetch_kernel,
        out_shape=(
            jax.ShapeDtypeStruct((32, 2, 512, DH), jnp.bfloat16),
            jax.ShapeDtypeStruct((8, 2, 512, DH), jnp.bfloat16),
            jax.ShapeDtypeStruct((8, 8, 128), jnp.float32),
        ),
        in_specs=[pl.BlockSpec(memory_space=pltpu.MemorySpace.HBM)] * 5,
        out_specs=(anywhere, anywhere, vmem),
        scratch_shapes=[
            pltpu.VMEM((4, 4, 512, DH), jnp.bfloat16),
            pltpu.VMEM((4, 8, 128), jnp.float32),
            pltpu.VMEM((512, 1024), jnp.bfloat16),
            pltpu.VMEM((512, 1024), jnp.bfloat16),
            dma((96,)),
            dma((7,)),
            dma((3, 4, 2)),
            dma((2, 4, 2)),
            dma((4, 4)),
            dma((4, 4, 2)),
            dma((4,)),
        ],
        compiler_params=pltpu.CompilerParams(
            collective_id=0, has_side_effects=True, vmem_limit_bytes=FETCH_VMEM
        ),
    )(*(pltpu.with_memory_space_constraint(a, pltpu.MemorySpace.HBM) for a in (k, v, q, g, o)))


def give_kernel(
    dq_ref, dkv_ref, out_ref,
    part, near, far,
    send, local, from_core, from_pair, from_all,
):
    s = lax.axis_index("seq")
    y = lax.axis_index("head")
    z, x, c = s // 8, s // 2 % 4, s % 2
    zhi = z // 2
    mirror, pair, core = 3 - z, z + 1 - 2 * (z % 2), 1 - c
    to_pair = {"seq": index(pair, x, c), "head": y}
    to_core = {"seq": index(z, x, core), "head": y}
    order = (1, 3, 2, 0)

    def owner(m, r, t):
        return {"seq": index(mirror if m else z, x + r, c), "head": (y + t) % 4}

    peers = [
        owner(m, r, t) for m in (0, 1) for r in range(4) for t in range(4) if (m, r, t) != (0, 0, 0)
    ]
    mover = Mover(send, local)
    push, move = mover.push, mover.move
    classes = (3 - pair, pair, mirror, z)
    units = [(cls, r, a) for cls in range(4) for r in order for a in (0, 1)]
    kept = []

    def spread(m, r, src, kind):
        col = pl.ds(pl.multiple_of(y * 1024 + (x * 2 + zhi) * DH, DH), DH)
        for t in order:
            rows = pl.ds(pl.multiple_of((y + t) % 4 * 128, 128), 128)
            piece, dst = src.at[rows], out_ref.at[kind, :, col]
            if (m, r, t) == (0, 0, 0):
                kept.append(move(piece, dst))
            else:
                push(piece, dst, from_all.at[kind, m, r, t], owner(m, r, t))

    def add(dst, terms):
        @pl.loop(0, 4)
        def _(i):
            rows = pl.ds(pl.multiple_of(i * 128, 128), 128)
            total = terms[0][rows, :].astype(jnp.float32)
            for term in terms[1:]:
                total += term[rows, :].astype(jnp.float32)
            dst[rows, :] = total.astype(jnp.bfloat16)

    loads = {}
    for cls in range(4):
        for r in order:
            at = index(classes[cls], x + r, c)
            loads[cls, r] = move(dkv_ref.at[at], part.at[cls, r])
    greet([to_core, to_pair] + peers)

    def cross(cls, r, a):
        away = index(classes[cls], x + r, core)
        push(dkv_ref.at[away, a], near.at[cls, r, a], from_core.at[cls, r, a], to_core)

    for unit in units[:16]:
        cross(*unit)
    for cls, r, a in units[:16]:
        if a == 0:
            loads[cls, r].wait()
        mover.arrived(near.at[cls, r, a], from_core.at[cls, r, a], to_core)
        mine = part.at[cls, r, a]
        add(mine, (mine, near.at[cls, r, a]))
        push(mine, far.at[cls, r, a], from_pair.at[cls, r, a], to_pair)
        if (cls, r, a) == units[3]:
            for unit in units[16:]:
                cross(*unit)
            for m in (1, 0):
                for rr in order:
                    spread(m, rr, dq_ref.at[m * 4 + (x + rr) % 4], 0)
    for cls, r, a in units[16:]:
        if a == 0:
            loads[cls, r].wait()
        mover.arrived(near.at[cls, r, a], from_core.at[cls, r, a], to_core)
        mover.arrived(far.at[cls - 2, r, a], from_pair.at[cls - 2, r, a], to_pair)
        mine = part.at[cls, r, a]
        add(mine, (mine, near.at[cls, r, a], far.at[cls - 2, r, a]))
        spread(3 - cls, r, mine, 1 + a)
    for m in (0, 1):
        for r in range(4):
            for t in range(4):
                if (m, r, t) == (0, 0, 0):
                    continue
                from_head = (x + 4 - r) % 4 * 2 + (1 - zhi if m else zhi)
                col = pl.multiple_of((y + 4 - t) % 4 * 1024 + from_head * DH, DH)
                for kind in range(3):
                    piece = out_ref.at[kind, :, pl.ds(col, DH)]
                    mover.arrived(piece, from_all.at[kind, m, r, t], to_core)
    for copy in kept:
        copy.wait()
    for copy in mover.sent:
        copy.wait_send()


def give(dq, dkv):
    anywhere = pl.BlockSpec(memory_space=pl.ANY)
    dma = pltpu.SemaphoreType.DMA
    return pl.pallas_call(
        give_kernel,
        out_shape=jax.ShapeDtypeStruct((3, 128, 4096), jnp.bfloat16),
        in_specs=[anywhere] * 2,
        out_specs=anywhere,
        scratch_shapes=[
            pltpu.VMEM((4, 4, 2, 512, DH), jnp.bfloat16),
            pltpu.VMEM((4, 4, 2, 512, DH), jnp.bfloat16),
            pltpu.VMEM((2, 4, 2, 512, DH), jnp.bfloat16),
            dma((144,)),
            dma((19,)),
            dma((4, 4, 2)),
            dma((2, 4, 2)),
            dma((3, 2, 4, 4)),
        ],
        compiler_params=pltpu.CompilerParams(
            collective_id=1, has_side_effects=True, vmem_limit_bytes=GIVE_VMEM
        ),
    )(dq, dkv)


def attend_kernel(
    rand, glob, qg_ref, rd_ref, kv_ref, dq_ref, dkv_ref,
    tab, edge, acc_ref, s0, s1, w0, w1, d0, d1, p0, p1,
):
    s = lax.axis_index("seq")
    z, x, c = s // 8, s // 2 % 4, s % 2
    head = x * 2 + z // 2

    def slot(block):
        return 2 * block - block % 8

    @pl.loop(0, 32)
    def _(i):
        acc_ref[pl.ds(i * 16, 16)] = jnp.zeros((16, BS, DH), jnp.float32)
        shard = jnp.where(i < 16, z, 3 - z) * 8 + i // 4 % 4 * 2 + c
        for u in range(2):
            block = shard * 8 + i % 4 * 2 + u
            at = i * 2 + u
            tab[at * 8] = slot(jnp.maximum(block - 1, 0))
            tab[at * 8 + 1] = slot(block)
            tab[at * 8 + 2] = slot(jnp.minimum(block + 1, 255))
            for j in range(3):
                tab[at * 8 + 3 + j] = slot(rand[j, head, block])
            for j in range(2):
                tab[at * 8 + 6 + j] = slot(glob[j])
            edge[at] = jnp.where(block == 0, 1, jnp.where(block == 255, 2, 0))

    first = lax.broadcasted_iota(jnp.int32, (1, 2 * BS), 1) < BS
    half = z // 2 * 4

    def slots_of(p):
        return [tab[p * 16 + j] for j in range(16)]

    def base_of(p):
        return p // 4 * 16 + p % 4 * 2

    def pair_rows(base):
        a, b = qg_ref[base], qg_ref[base + 1]
        zero = jnp.zeros_like(a)
        return jnp.concatenate(
            [jnp.concatenate([a, zero], axis=1), jnp.concatenate([zero, b], axis=1)], axis=0
        )

    def pair_keys(slots, offset):
        return jnp.concatenate(
            [
                jnp.concatenate([kv_ref[slots[j] + offset], kv_ref[slots[8 + j] + offset]], axis=1)
                for j in range(8)
            ],
            axis=0,
        )

    def score(p, s_ref, w_ref):
        slots, base = slots_of(p), base_of(p)
        s_ref[...] = dot(pair_keys(slots, 0), pair_rows(base), NT)
        w_ref[...] = dot(pair_keys(slots, 8), pair_rows(base + 8), NT)

    def soften(p, s_ref, w_ref, d_ref, p_ref):
        state = jnp.where(first, edge[2 * p], edge[2 * p + 1])
        low = jnp.where(state == 1, -jnp.inf, 0.0)
        high = jnp.where(state == 2, -jnp.inf, 0.0)
        s = s_ref[...] * SCALE_LOG2E
        s = jnp.concatenate(
            [s[:BS] + low, s[BS : 2 * BS], s[2 * BS : 3 * BS] + high, s[3 * BS :]], axis=0
        )
        e = jnp.exp2(s - jnp.max(s, axis=0, keepdims=True))
        weights = e * (1.0 / jnp.sum(e, axis=0, keepdims=True))
        p_ref[...] = weights.astype(jnp.bfloat16)
        rd = rd_ref[p // 4, pl.ds(half + p % 4, 1), :]
        d_ref[...] = (weights * (w_ref[...] - rd)).astype(jnp.bfloat16)

    def spread(p, d_ref, p_ref):
        slots, base = slots_of(p), base_of(p)
        d = d_ref[...]
        dq = dot(d, pair_keys(slots, 0), TN) * SCALE
        dq_ref[2 * p] = dq[:BS, :DH].astype(jnp.bfloat16)
        dq_ref[2 * p + 1] = dq[BS:, DH:].astype(jnp.bfloat16)
        dk = dot(d, pair_rows(base), NN)
        dv = dot(p_ref[...], pair_rows(base + 8), NN)
        for j in range(16):
            side, row = j // 8 * DH, j % 8 * BS
            acc_ref[slots[j]] += dk[row : row + BS, side : side + DH]
            acc_ref[slots[j] + 8] += dv[row : row + BS, side : side + DH]

    score(0, s0, w0)
    soften(0, s0, w0, d0, p0)
    score(1, s1, w1)

    @pl.loop(1, 16)
    def _(t):
        a = 2 * t
        spread(a - 2, d0, p0)
        soften(a - 1, s1, w1, d1, p1)
        score(a, s0, w0)
        spread(a - 1, d1, p1)
        soften(a, s0, w0, d0, p0)
        score(a + 1, s1, w1)

    soften(31, s1, w1, d1, p1)
    spread(30, d0, p0)
    spread(31, d1, p1)

    @pl.loop(0, 32)
    def _(t):
        keys, values = pl.ds(t * 16, 8), pl.ds(t * 16 + 8, 8)
        dkv_ref[keys] = (acc_ref[keys] * SCALE).astype(jnp.bfloat16)
        dkv_ref[values] = acc_ref[values].astype(jnp.bfloat16)


def attend(rand, glob, qg, rd, kv):
    vmem = pl.BlockSpec(memory_space=pltpu.VMEM)
    smem = pl.BlockSpec(memory_space=pltpu.SMEM)
    return pl.pallas_call(
        attend_kernel,
        out_shape=(
            jax.ShapeDtypeStruct((64, BS, DH), jnp.bfloat16),
            jax.ShapeDtypeStruct((512, BS, DH), jnp.bfloat16),
        ),
        in_specs=[smem, smem, vmem, vmem, vmem],
        out_specs=(vmem, vmem),
        scratch_shapes=[
            pltpu.SMEM((512,), jnp.int32),
            pltpu.SMEM((64,), jnp.int32),
            pltpu.VMEM((512, BS, DH), jnp.float32),
        ]
        + [pltpu.VMEM((8 * BS, 2 * BS), jnp.float32)] * 4
        + [pltpu.VMEM((8 * BS, 2 * BS), jnp.bfloat16)] * 4,
        compiler_params=pltpu.CompilerParams(vmem_limit_bytes=ATTEND_VMEM),
    )(rand, glob, qg, rd, kv)


def on_device(
    queries, key_states, value_states, forward_out, grad_out, random_blocks, global_blocks
):
    kv, qg, rd = fetch(key_states, value_states, queries, grad_out, forward_out)
    dq, dkv = attend(
        random_blocks.transpose(2, 1, 0),
        global_blocks,
        qg.reshape(128, BS, DH),
        rd,
        kv.reshape(512, BS, DH),
    )
    outs = give(dq.reshape(8, 512, DH), dkv.reshape(32, 2, 512, DH))
    return outs[0], outs[1], outs[2]


def solution(mesh):
    return jax.shard_map(
        on_device,
        mesh=mesh,
        in_specs=(
            P("seq", "head"),
            P("seq", "head"),
            P("seq", "head"),
            P("seq", "head"),
            P("seq", "head"),
            P(None, "head", None),
            P(),
        ),
        out_specs=(P(("seq", "head"), None), P(("seq", "head"), None), P(("seq", "head"), None)),
        check_vma=False,
    )
```

time: 165 us -> 139 us (0.84)
  Pallas kernels: 158 us -> 137 us
  local copies, waits for them, and re-layouts: 4.8 us -> 1.76 us
    pallas_call x1, Pallas kernels: 70.2 us -> 53.3 us  [fetch(): pl.pallas_call(fetch_kernel, out_shape=(jax.ShapeDtypeStruct((32, 2, 512,...]
    pallas_call x1, Pallas kernels: 23.2 us -> 19 us  [attend(): pl.pallas_call(attend_kernel, out_shape=(jax.ShapeDtypeStruct((64, BS, DH...]
    squeeze x1, local copies, waits for them, and re-layouts: 3.61 us -> 1.75 us  [on_device(): return (outs[0], outs[1], outs[2])]
where the time goes in v5:
time: 139 us
  Pallas kernels  137 us (99%)
  local copies, waits for them, and re-layouts  1.76 us (1%)
    pallas_call x1, Pallas kernels, give(): pl.pallas_call(give_kernel, out_shape=jax.ShapeDtypeStruct((3, 128, 4096)...  64.6 us
    pallas_call x1, Pallas kernels, fetch(): pl.pallas_call(fetch_kernel, out_shape=(jax.ShapeDtypeStruct((32, 2, 512,...  53.3 us
    pallas_call x1, Pallas kernels, attend(): pl.pallas_call(attend_kernel, out_shape=(jax.ShapeDtypeStruct((64, BS, DH...  19 us

profile of v5, /device:TPU:33, one launch (start us, length us, event | category | flops | bytes accessed | tf_op | source)
XLA Modules:
  0.0 139.3 jit_solution(17532692500267989564)
XLA Ops:
  0.6 0.0 copy-start.1
  0.6 0.0 copy-start
  0.7 53.3 %shard_map.94 = (bf16[32,2,512,128]{3,2,1,0:T(8,128)(2,1)S(1)}, bf16[8,2,512,128]{3,2,1,0:T(8,128)(2,1)S(1)}, f32[8,8,128]{2,1,0:T(8,128)S(1)}) custom-call(bf16[512,1024]{1,0:T(8,128)(2,1)} %k_ref.1, bf16[512,1024]{1,0:T(8,128)(2,1)} %v_ref.1, bf16[512,1024]{1,0:T(8,128)(2,1)} %q_ref.1, bf16[512,1024]{1,0:T(8,128)(2,1)} %g_ref.1, bf16[512,1024]{1,0:T(8,128)(2,1)} %o_ref.1), custom_call_target="tpu_custom_call" | custom-call | tf_op jit(solution)/shard_map/pallas_call | solution.py:239
  53.9 0.0 copy-done.1
  53.9 0.0 copy-done
  54.0 19.0 %shard_map.95 = (bf16[64,64,128]{2,1,0:T(8,128)(2,1)S(1)}, bf16[512,64,128]{2,1,0:T(8,128)(2,1)S(1)}) custom-call(s32[3,8,256]{2,1,0:T(8,128)S(1)} %bitcast.15, s32[2]{0:T(128)S(1)} %copy-done.1, bf16[128,64,128]{2,1,0:T(8,128)(2,1)S(1)} %bitcast.13, f32[8,8,128]{2,1,0:T(8,128)S(1)} %get-tuple-element.9.rd_ref, bf16[512,64,128]{2,1,0:T(8,128)(2,1)S(1)} %bitcast.12), custom_call_target="tpu_custom_call" | custom-call | tf_op jit(solution)/shard_map/pallas_call | solution.py:498
  73.0 64.6 %shard_map.96 = bf16[3,128,4096]{2,1,0:T(8,128)(2,1)S(1)} custom-call(bf16[8,512,128]{2,1,0:T(8,128)(2,1)S(1)} %bitcast.14, bf16[32,2,512,128]{3,2,1,0:T(8,128)(2,1)S(1)} %bitcast.11), custom_call_target="tpu_custom_call" | custom-call | tf_op jit(solution)/shard_map/pallas_call | solution.py:365
  137.6 1.8 %slice_bitcast_fusion = (bf16[128,4096]{1,0:T(8,128)(2,1)}, bf16[128,4096]{1,0:T(8,128)(2,1)}, bf16[128,4096]{1,0:T(8,128)(2,1)}) fusion(bf16[3,128,4096]{2,1,0:T(8,128)(2,1)S(1)} %shard_map.96), kind=kLoop, calls=%fused_computation | loop fusion | bytes 6291456 | tf_op jit(solution)/shard_map/squeeze | solution.py:529
Async XLA Ops:
  0.6 53.3 %copy-start.1 = (s32[2]{0:T(128)S(1)}, s32[2]{0:T(128)}, u32[]{:S(2)}) copy-start(s32[2]{0:T(128)} %glob.1) | copy-start | bytes 28
  0.6 53.3 %copy-start = (s32[256,8,3]{0,1,2:T(8,128)S(1)}, s32[256,8,3]{0,1,2:T(8,128)}, u32[]{:S(2)}) copy-start(s32[256,8,3]{0,1,2:T(8,128)} %param.12) | copy-start | bytes 73732

commit v6 on v5

--- a/solution.py
+++ b/solution.py
@@ -9,9 +9,9 @@
 BS = 64
 SCALE = DH**-0.5
 SCALE_LOG2E = SCALE * 1.4426950408889634
-ATTEND_VMEM = 24 * 1024 * 1024
+ATTEND_VMEM = 8 * 1024 * 1024
 FETCH_VMEM = 10 * 1024 * 1024
-GIVE_VMEM = 16 * 1024 * 1024
+GIVE_VMEM = 20 * 1024 * 1024
 NT = (((1,), (1,)), ((), ()))
 TN = (((0,), (0,)), ((), ()))
 NN = (((1,), (0,)), ((), ()))
@@ -62,16 +62,19 @@
         return copy
 
 
-def greet(peers):
+def welcome(peers):
     barrier = pltpu.get_barrier_semaphore()
     for peer in peers:
         pl.semaphore_signal(barrier, inc=1, device_id=peer, device_id_type=MESH)
-    pl.semaphore_wait(barrier, len(peers))
+
+
+def enter(peers):
+    pl.semaphore_wait(pltpu.get_barrier_semaphore(), len(peers))
 
 
 def fetch_kernel(
     k_ref, v_ref, q_ref, g_ref, o_ref,
-    kv_out, qg_out, rd_out,
+    kv_out, qg_out, rd_out, zeros,
     oth, rd_mine, g_all, o_all,
     send, local, from_x, from_pair, from_mirror, from_core, from_rd,
 ):
@@ -130,7 +133,8 @@
         push(piece, piece, from_core.at[2 + m, r, a], to_core)
 
     dots = [move(g_ref, g_all), move(o_ref, o_all)]
-    greet(along_x[1:] + [to_mirror, to_pair, to_core])
+    welcome(along_x[1:] + [to_mirror, to_pair, to_core])
+    enter(along_x[1:] + [to_mirror, to_pair, to_core])
     for a in (0, 1):
         push(head(a, x, zhi), at(z, 0, a), from_pair.at[0, 0, a], to_pair)
         push(head(a, x, 1 - zhi), at(z, 0, a), from_mirror.at[0, a], to_mirror)
@@ -211,6 +215,11 @@
     paired(1, 1, 0)
     other(2, 2)
     other(2, 3)
+
+    @pl.loop(0, 32)
+    def _(i):
+        zeros[pl.ds(i * 16, 16)] = jnp.zeros((16, BS, DH), jnp.float32)
+
     paired(1, 3, 1)
     paired(0, 2, 0)
     paired(1, 1, 1)
@@ -242,9 +251,10 @@
             jax.ShapeDtypeStruct((32, 2, 512, DH), jnp.bfloat16),
             jax.ShapeDtypeStruct((8, 2, 512, DH), jnp.bfloat16),
             jax.ShapeDtypeStruct((8, 8, 128), jnp.float32),
+            jax.ShapeDtypeStruct((512, BS, DH), jnp.float32),
         ),
         in_specs=[pl.BlockSpec(memory_space=pltpu.MemorySpace.HBM)] * 5,
-        out_specs=(anywhere, anywhere, vmem),
+        out_specs=(anywhere, anywhere, vmem, vmem),
         scratch_shapes=[
             pltpu.VMEM((4, 4, 512, DH), jnp.bfloat16),
             pltpu.VMEM((4, 8, 128), jnp.float32),
@@ -265,8 +275,8 @@
 
 
 def give_kernel(
-    dq_ref, dkv_ref, out_ref,
-    part, near, far,
+    dq_ref, acc_ref, out_ref,
+    part, away, near, far,
     send, local, from_core, from_pair, from_all,
 ):
     s = lax.axis_index("seq")
@@ -276,7 +286,7 @@
     mirror, pair, core = 3 - z, z + 1 - 2 * (z % 2), 1 - c
     to_pair = {"seq": index(pair, x, c), "head": y}
     to_core = {"seq": index(z, x, core), "head": y}
-    order = (1, 3, 2, 0)
+    order = (2, 1, 3, 0)
 
     def owner(m, r, t):
         return {"seq": index(mirror if m else z, x + r, c), "head": (y + t) % 4}
@@ -300,48 +310,48 @@
             else:
                 push(piece, dst, from_all.at[kind, m, r, t], owner(m, r, t))
 
-    def add(dst, terms):
+    def add(dst, slot, a, terms):
         @pl.loop(0, 4)
         def _(i):
             rows = pl.ds(pl.multiple_of(i * 128, 128), 128)
-            total = terms[0][rows, :].astype(jnp.float32)
-            for term in terms[1:]:
+            total = acc_ref[slot, a, rows, :]
+            if a == 0:
+                total *= SCALE
+            for term in terms:
                 total += term[rows, :].astype(jnp.float32)
             dst[rows, :] = total.astype(jnp.bfloat16)
 
-    loads = {}
-    for cls in range(4):
-        for r in order:
-            at = index(classes[cls], x + r, c)
-            loads[cls, r] = move(dkv_ref.at[at], part.at[cls, r])
-    greet([to_core, to_pair] + peers)
+    def leave(cls, r, a):
+        add(away.at[cls, r, a], index(classes[cls], x + r, core), a, ())
 
     def cross(cls, r, a):
-        away = index(classes[cls], x + r, core)
-        push(dkv_ref.at[away, a], near.at[cls, r, a], from_core.at[cls, r, a], to_core)
-
+        sem = from_core.at[cls, r, a]
+        push(away.at[cls, r, a], near.at[cls, r, a], sem, to_core)
+
+    welcome([to_core, to_pair] + peers)
+    for unit in units[:16]:
+        leave(*unit)
+    enter([to_core, to_pair] + peers)
     for unit in units[:16]:
         cross(*unit)
     for cls, r, a in units[:16]:
-        if a == 0:
-            loads[cls, r].wait()
         mover.arrived(near.at[cls, r, a], from_core.at[cls, r, a], to_core)
         mine = part.at[cls, r, a]
-        add(mine, (mine, near.at[cls, r, a]))
+        add(mine, index(classes[cls], x + r, c), a, (near.at[cls, r, a],))
         push(mine, far.at[cls, r, a], from_pair.at[cls, r, a], to_pair)
         if (cls, r, a) == units[3]:
-            for unit in units[16:]:
-                cross(*unit)
             for m in (1, 0):
                 for rr in order:
                     spread(m, rr, dq_ref.at[m * 4 + (x + rr) % 4], 0)
+            for unit in units[16:]:
+                leave(*unit)
+                cross(*unit)
     for cls, r, a in units[16:]:
-        if a == 0:
-            loads[cls, r].wait()
         mover.arrived(near.at[cls, r, a], from_core.at[cls, r, a], to_core)
         mover.arrived(far.at[cls - 2, r, a], from_pair.at[cls - 2, r, a], to_pair)
         mine = part.at[cls, r, a]
-        add(mine, (mine, near.at[cls, r, a], far.at[cls - 2, r, a]))
+        terms = (near.at[cls, r, a], far.at[cls - 2, r, a])
+        add(mine, index(classes[cls], x + r, c), a, terms)
         spread(3 - cls, r, mine, 1 + a)
     for m in (0, 1):
         for r in range(4):
@@ -359,20 +369,21 @@
         copy.wait_send()
 
 
-def give(dq, dkv):
+def give(dq, acc):
     anywhere = pl.BlockSpec(memory_space=pl.ANY)
     dma = pltpu.SemaphoreType.DMA
     return pl.pallas_call(
         give_kernel,
         out_shape=jax.ShapeDtypeStruct((3, 128, 4096), jnp.bfloat16),
-        in_specs=[anywhere] * 2,
+        in_specs=[anywhere, pl.BlockSpec(memory_space=pltpu.VMEM)],
         out_specs=anywhere,
         scratch_shapes=[
             pltpu.VMEM((4, 4, 2, 512, DH), jnp.bfloat16),
             pltpu.VMEM((4, 4, 2, 512, DH), jnp.bfloat16),
+            pltpu.VMEM((4, 4, 2, 512, DH), jnp.bfloat16),
             pltpu.VMEM((2, 4, 2, 512, DH), jnp.bfloat16),
             dma((144,)),
-            dma((19,)),
+            dma((3,)),
             dma((4, 4, 2)),
             dma((2, 4, 2)),
             dma((3, 2, 4, 4)),
@@ -380,41 +391,30 @@
         compiler_params=pltpu.CompilerParams(
             collective_id=1, has_side_effects=True, vmem_limit_bytes=GIVE_VMEM
         ),
-    )(dq, dkv)
+    )(dq, acc)
 
 
 def attend_kernel(
-    rand, glob, qg_ref, rd_ref, kv_ref, dq_ref, dkv_ref,
-    tab, edge, acc_ref, s0, s1, w0, w1, d0, d1, p0, p1,
+    rand, glob, qg_ref, rd_ref, kv_ref, zeros_ref, dq_ref, acc_ref,
+    s0, s1, w0, w1, d0, d1, p0, p1,
 ):
     s = lax.axis_index("seq")
     z, x, c = s // 8, s // 2 % 4, s % 2
     head = x * 2 + z // 2
-
-    def slot(block):
-        return 2 * block - block % 8
-
-    @pl.loop(0, 32)
-    def _(i):
-        acc_ref[pl.ds(i * 16, 16)] = jnp.zeros((16, BS, DH), jnp.float32)
-        shard = jnp.where(i < 16, z, 3 - z) * 8 + i // 4 % 4 * 2 + c
-        for u in range(2):
-            block = shard * 8 + i % 4 * 2 + u
-            at = i * 2 + u
-            tab[at * 8] = slot(jnp.maximum(block - 1, 0))
-            tab[at * 8 + 1] = slot(block)
-            tab[at * 8 + 2] = slot(jnp.minimum(block + 1, 255))
-            for j in range(3):
-                tab[at * 8 + 3 + j] = slot(rand[j, head, block])
-            for j in range(2):
-                tab[at * 8 + 6 + j] = slot(glob[j])
-            edge[at] = jnp.where(block == 0, 1, jnp.where(block == 255, 2, 0))
-
     first = lax.broadcasted_iota(jnp.int32, (1, 2 * BS), 1) < BS
     half = z // 2 * 4
 
+    def block_of(p):
+        shard = jnp.where(p < 16, z, 3 - z) * 8 + p // 4 % 4 * 2 + c
+        return shard * 8 + p % 4 * 2
+
     def slots_of(p):
-        return [tab[p * 16 + j] for j in range(16)]
+        slots = []
+        for block in (block_of(p), block_of(p) + 1):
+            named = [jnp.maximum(block - 1, 0), block, jnp.minimum(block + 1, 255)]
+            named += [rand[j, head, block] for j in range(3)] + [glob[0], glob[1]]
+            slots += [2 * b - b % 8 for b in named]
+        return slots
 
     def base_of(p):
         return p // 4 * 16 + p % 4 * 2
@@ -441,9 +441,8 @@
         w_ref[...] = dot(pair_keys(slots, 8), pair_rows(base + 8), NT)
 
     def soften(p, s_ref, w_ref, d_ref, p_ref):
-        state = jnp.where(first, edge[2 * p], edge[2 * p + 1])
-        low = jnp.where(state == 1, -jnp.inf, 0.0)
-        high = jnp.where(state == 2, -jnp.inf, 0.0)
+        low = jnp.where(first & (block_of(p) == 0), -jnp.inf, 0.0)
+        high = jnp.where(~first & (block_of(p) == 254), -jnp.inf, 0.0)
         s = s_ref[...] * SCALE_LOG2E
         s = jnp.concatenate(
             [s[:BS] + low, s[BS : 2 * BS], s[2 * BS : 3 * BS] + high, s[3 * BS :]], axis=0
@@ -485,47 +484,44 @@
     spread(30, d0, p0)
     spread(31, d1, p1)
 
-    @pl.loop(0, 32)
-    def _(t):
-        keys, values = pl.ds(t * 16, 8), pl.ds(t * 16 + 8, 8)
-        dkv_ref[keys] = (acc_ref[keys] * SCALE).astype(jnp.bfloat16)
-        dkv_ref[values] = acc_ref[values].astype(jnp.bfloat16)
-
-
-def attend(rand, glob, qg, rd, kv):
+
+def attend(rand, glob, qg, rd, kv, zeros):
     vmem = pl.BlockSpec(memory_space=pltpu.VMEM)
     smem = pl.BlockSpec(memory_space=pltpu.SMEM)
     return pl.pallas_call(
         attend_kernel,
         out_shape=(
             jax.ShapeDtypeStruct((64, BS, DH), jnp.bfloat16),
-            jax.ShapeDtypeStruct((512, BS, DH), jnp.bfloat16),
+            jax.ShapeDtypeStruct((512, BS, DH), jnp.float32),
         ),
-        in_specs=[smem, smem, vmem, vmem, vmem],
+        in_specs=[smem, smem, vmem, vmem, vmem, vmem],
         out_specs=(vmem, vmem),
-        scratch_shapes=[
-            pltpu.SMEM((512,), jnp.int32),
-            pltpu.SMEM((64,), jnp.int32),
-            pltpu.VMEM((512, BS, DH), jnp.float32),
-        ]
-        + [pltpu.VMEM((8 * BS, 2 * BS), jnp.float32)] * 4
+        input_output_aliases={5: 1},
+        scratch_shapes=[pltpu.VMEM((8 * BS, 2 * BS), jnp.float32)] * 4
         + [pltpu.VMEM((8 * BS, 2 * BS), jnp.bfloat16)] * 4,
         compiler_params=pltpu.CompilerParams(vmem_limit_bytes=ATTEND_VMEM),
-    )(rand, glob, qg, rd, kv)
+    )(
+        *(pltpu.with_memory_space_constraint(a, pltpu.MemorySpace.HBM) for a in (rand, glob)),
+        qg,
+        rd,
+        kv,
+        zeros,
+    )
 
 
 def on_device(
     queries, key_states, value_states, forward_out, grad_out, random_blocks, global_blocks
 ):
-    kv, qg, rd = fetch(key_states, value_states, queries, grad_out, forward_out)
-    dq, dkv = attend(
+    kv, qg, rd, zeros = fetch(key_states, value_states, queries, grad_out, forward_out)
+    dq, acc = attend(
         random_blocks.transpose(2, 1, 0),
         global_blocks,
         qg.reshape(128, BS, DH),
         rd,
         kv.reshape(512, BS, DH),
+        zeros,
     )
-    outs = give(dq.reshape(8, 512, DH), dkv.reshape(32, 2, 512, DH))
+    outs = give(dq.reshape(8, 512, DH), acc.reshape(32, 2, 512, DH))
     return outs[0], outs[1], outs[2]
 
 

time: 139 us -> 135 us (0.971)
  Pallas kernels: 137 us -> 133 us
    pallas_call x1, Pallas kernels: 19 us -> 15.5 us  [attend(): pl.pallas_call(attend_kernel, out_shape=(jax.ShapeDtypeStruct((64, BS, DH...]
where the time goes in v6:
time: 135 us
  Pallas kernels  133 us (99%)
  local copies, waits for them, and re-layouts  1.75 us (1%)
    pallas_call x1, Pallas kernels, give(): pl.pallas_call(give_kernel, out_shape=jax.ShapeDtypeStruct((3, 128, 4096)...  63.9 us
    pallas_call x1, Pallas kernels, fetch(): pl.pallas_call(fetch_kernel, out_shape=(jax.ShapeDtypeStruct((32, 2, 512,...  53.3 us
    pallas_call x1, Pallas kernels, attend(): pl.pallas_call(attend_kernel, out_shape=(jax.ShapeDtypeStruct((64, BS, DH...  15.5 us

profile of v6, /device:TPU:33, one launch (start us, length us, event | category | flops | bytes accessed | tf_op | source)
XLA Modules:
  0.0 135.0 jit_solution(6580911649174950590)
XLA Ops:
  0.6 53.3 %shard_map.94 = (bf16[32,2,512,128]{3,2,1,0:T(8,128)(2,1)S(1)}, bf16[8,2,512,128]{3,2,1,0:T(8,128)(2,1)S(1)}, f32[8,8,128]{2,1,0:T(8,128)S(1)}, f32[512,64,128]{2,1,0:T(8,128)S(1)}) custom-call(bf16[512,1024]{1,0:T(8,128)(2,1)} %k_ref.1, bf16[512,1024]{1,0:T(8,128)(2,1)} %v_ref.1, bf16[512,1024]{1,0:T(8,128)(2,1)} %q_ref.1, bf16[512,1024]{1,0:T(8,128)(2,1)} %g_ref.1, ...), custom_call_target="tpu_custom_call" | custom-call | tf_op jit(solution)/shard_map/pallas_call | solution.py:248
  53.9 15.5 %shard_map.95 = (bf16[64,64,128]{2,1,0:T(8,128)(2,1)S(1)}, f32[512,64,128]{2,1,0:T(8,128)S(1)}) custom-call(s32[3,8,256]{2,1,0:T(8,128)} %bitcast.15, s32[2]{0:T(128)} %glob.1, bf16[128,64,128]{2,1,0:T(8,128)(2,1)S(1)} %bitcast.13, f32[8,8,128]{2,1,0:T(8,128)S(1)} %get-tuple-element.10.rd_ref, ...), custom_call_target="tpu_custom_call", output_to_operand_aliasing={{1}: (5, {})} | custom-call | tf_op jit(solution)/shard_map/pallas_call | solution.py:491
  69.4 63.9 %shard_map.96 = bf16[3,128,4096]{2,1,0:T(8,128)(2,1)S(1)} custom-call(bf16[8,512,128]{2,1,0:T(8,128)(2,1)S(1)} %bitcast.14, f32[32,2,512,128]{3,2,1,0:T(8,128)S(1)} %bitcast.11), custom_call_target="tpu_custom_call" | custom-call | tf_op jit(solution)/shard_map/pallas_call | solution.py:375
  133.3 1.8 %slice_bitcast_fusion = (bf16[128,4096]{1,0:T(8,128)(2,1)}, bf16[128,4096]{1,0:T(8,128)(2,1)}, bf16[128,4096]{1,0:T(8,128)(2,1)}) fusion(bf16[3,128,4096]{2,1,0:T(8,128)(2,1)S(1)} %shard_map.96), kind=kLoop, calls=%fused_computation | loop fusion | bytes 6291456 | tf_op jit(solution)/shard_map/squeeze | solution.py:525

commit v7 on v6

--- a/solution.py
+++ b/solution.py
@@ -277,7 +277,7 @@
 def give_kernel(
     dq_ref, acc_ref, out_ref,
     part, away, near, far,
-    send, local, from_core, from_pair, from_all,
+    send, local, from_core, from_pair, from_last, from_all,
 ):
     s = lax.axis_index("seq")
     y = lax.axis_index("head")
@@ -300,26 +300,34 @@
     units = [(cls, r, a) for cls in range(4) for r in order for a in (0, 1)]
     kept = []
 
+    def quarter(t):
+        return pl.ds(pl.multiple_of((y + t) % 4 * 128, 128), 128)
+
+    def hand(m, r, t, src, kind):
+        col = pl.ds(pl.multiple_of(y * 1024 + (x * 2 + zhi) * DH, DH), DH)
+        piece, dst = src.at[quarter(t)], out_ref.at[kind, :, col]
+        if (m, r, t) == (0, 0, 0):
+            kept.append(move(piece, dst))
+        else:
+            push(piece, dst, from_all.at[kind, m, r, t], owner(m, r, t))
+
     def spread(m, r, src, kind):
-        col = pl.ds(pl.multiple_of(y * 1024 + (x * 2 + zhi) * DH, DH), DH)
         for t in order:
-            rows = pl.ds(pl.multiple_of((y + t) % 4 * 128, 128), 128)
-            piece, dst = src.at[rows], out_ref.at[kind, :, col]
-            if (m, r, t) == (0, 0, 0):
-                kept.append(move(piece, dst))
-            else:
-                push(piece, dst, from_all.at[kind, m, r, t], owner(m, r, t))
+            hand(m, r, t, src, kind)
+
+    def add_rows(dst, slot, a, rows, terms):
+        total = acc_ref[slot, a, rows, :]
+        if a == 0:
+            total *= SCALE
+        for term in terms:
+            total += term[rows, :].astype(jnp.float32)
+        dst[rows, :] = total.astype(jnp.bfloat16)
 
     def add(dst, slot, a, terms):
         @pl.loop(0, 4)
         def _(i):
             rows = pl.ds(pl.multiple_of(i * 128, 128), 128)
-            total = acc_ref[slot, a, rows, :]
-            if a == 0:
-                total *= SCALE
-            for term in terms:
-                total += term[rows, :].astype(jnp.float32)
-            dst[rows, :] = total.astype(jnp.bfloat16)
+            add_rows(dst, slot, a, rows, terms)
 
     def leave(cls, r, a):
         add(away.at[cls, r, a], index(classes[cls], x + r, core), a, ())
@@ -334,7 +342,7 @@
     enter([to_core, to_pair] + peers)
     for unit in units[:16]:
         cross(*unit)
-    for cls, r, a in units[:16]:
+    for cls, r, a in units[:14]:
         mover.arrived(near.at[cls, r, a], from_core.at[cls, r, a], to_core)
         mine = part.at[cls, r, a]
         add(mine, index(classes[cls], x + r, c), a, (near.at[cls, r, a],))
@@ -346,13 +354,28 @@
             for unit in units[16:]:
                 leave(*unit)
                 cross(*unit)
-    for cls, r, a in units[16:]:
+    for a in (0, 1):
+        mover.arrived(near.at[1, 0, a], from_core.at[1, 0, a], to_core)
+    for t in order:
+        for a in (0, 1):
+            mine, rows = part.at[1, 0, a], quarter(t)
+            add_rows(mine, index(pair, x, c), a, rows, (near.at[1, 0, a],))
+            push(mine.at[rows], far.at[1, 0, a, rows], from_last.at[a, t], to_pair)
+    for cls, r, a in units[16:30]:
         mover.arrived(near.at[cls, r, a], from_core.at[cls, r, a], to_core)
         mover.arrived(far.at[cls - 2, r, a], from_pair.at[cls - 2, r, a], to_pair)
         mine = part.at[cls, r, a]
         terms = (near.at[cls, r, a], far.at[cls - 2, r, a])
         add(mine, index(classes[cls], x + r, c), a, terms)
         spread(3 - cls, r, mine, 1 + a)
+    for a in (0, 1):
+        mover.arrived(near.at[3, 0, a], from_core.at[3, 0, a], to_core)
+    for t in order:
+        for a in (0, 1):
+            mine, rows = part.at[3, 0, a], quarter(t)
+            mover.arrived(far.at[1, 0, a, rows], from_last.at[a, t], to_pair)
+            add_rows(mine, index(z, x, c), a, rows, (near.at[3, 0, a], far.at[1, 0, a]))
+            hand(0, 0, t, mine, 1 + a)
     for m in (0, 1):
         for r in range(4):
             for t in range(4):
@@ -382,10 +405,11 @@
             pltpu.VMEM((4, 4, 2, 512, DH), jnp.bfloat16),
             pltpu.VMEM((4, 4, 2, 512, DH), jnp.bfloat16),
             pltpu.VMEM((2, 4, 2, 512, DH), jnp.bfloat16),
-            dma((144,)),
+            dma((148,)),
             dma((3,)),
             dma((4, 4, 2)),
             dma((2, 4, 2)),
+            dma((2, 4)),
             dma((3, 2, 4, 4)),
         ],
         compiler_params=pltpu.CompilerParams(

time: 135 us -> 133 us (0.985)
  Pallas kernels: 133 us -> 131 us
    pallas_call x1, Pallas kernels: 63.9 us -> 61.9 us  [give(): pl.pallas_call(give_kernel, out_shape=jax.ShapeDtypeStruct((3, 128, 4096)...]
where the time goes in v7:
time: 133 us
  Pallas kernels  131 us (98%)
  local copies, waits for them, and re-layouts  1.75 us (1%)
    pallas_call x1, Pallas kernels, give(): pl.pallas_call(give_kernel, out_shape=jax.ShapeDtypeStruct((3, 128, 4096)...  61.9 us
    pallas_call x1, Pallas kernels, fetch(): pl.pallas_call(fetch_kernel, out_shape=(jax.ShapeDtypeStruct((32, 2, 512,...  53.3 us
    pallas_call x1, Pallas kernels, attend(): pl.pallas_call(attend_kernel, out_shape=(jax.ShapeDtypeStruct((64, BS, DH...  15.5 us

profile of v7, /device:TPU:33, one launch (start us, length us, event | category | flops | bytes accessed | tf_op | source)
XLA Modules:
  0.0 133.0 jit_solution(15557209766512964479)
XLA Ops:
  0.6 53.3 %shard_map.94 = (bf16[32,2,512,128]{3,2,1,0:T(8,128)(2,1)S(1)}, bf16[8,2,512,128]{3,2,1,0:T(8,128)(2,1)S(1)}, f32[8,8,128]{2,1,0:T(8,128)S(1)}, f32[512,64,128]{2,1,0:T(8,128)S(1)}) custom-call(bf16[512,1024]{1,0:T(8,128)(2,1)} %k_ref.1, bf16[512,1024]{1,0:T(8,128)(2,1)} %v_ref.1, bf16[512,1024]{1,0:T(8,128)(2,1)} %q_ref.1, bf16[512,1024]{1,0:T(8,128)(2,1)} %g_ref.1, ...), custom_call_target="tpu_custom_call" | custom-call | tf_op jit(solution)/shard_map/pallas_call | solution.py:248
  53.9 15.5 %shard_map.95 = (bf16[64,64,128]{2,1,0:T(8,128)(2,1)S(1)}, f32[512,64,128]{2,1,0:T(8,128)S(1)}) custom-call(s32[3,8,256]{2,1,0:T(8,128)} %bitcast.15, s32[2]{0:T(128)} %glob.1, bf16[128,64,128]{2,1,0:T(8,128)(2,1)S(1)} %bitcast.13, f32[8,8,128]{2,1,0:T(8,128)S(1)} %get-tuple-element.10.rd_ref, ...), custom_call_target="tpu_custom_call", output_to_operand_aliasing={{1}: (5, {})} | custom-call | tf_op jit(solution)/shard_map/pallas_call | solution.py:515
  69.4 61.9 %shard_map.96 = bf16[3,128,4096]{2,1,0:T(8,128)(2,1)S(1)} custom-call(bf16[8,512,128]{2,1,0:T(8,128)(2,1)S(1)} %bitcast.14, f32[32,2,512,128]{3,2,1,0:T(8,128)S(1)} %bitcast.11), custom_call_target="tpu_custom_call" | custom-call | tf_op jit(solution)/shard_map/pallas_call | solution.py:398
  131.2 1.8 %slice_bitcast_fusion = (bf16[128,4096]{1,0:T(8,128)(2,1)}, bf16[128,4096]{1,0:T(8,128)(2,1)}, bf16[128,4096]{1,0:T(8,128)(2,1)}) fusion(bf16[3,128,4096]{2,1,0:T(8,128)(2,1)S(1)} %shard_map.96), kind=kLoop, calls=%fused_computation | loop fusion | bytes 6291456 | tf_op jit(solution)/shard_map/squeeze | solution.py:549

commit v8 on v7

--- a/solution.py
+++ b/solution.py
@@ -177,7 +177,7 @@
     for d in (1, 3, 2):
         for a in (2, 3):
             send_other(d, a)
-    for d in (1, 3, 2):
+    for d in (2, 1, 3):
         for a in (2, 3):
             send_own(d, a)
     other(3, 0)

time: 133 us -> 133 us (level)
  no operation moved by 1% of the time
where the time goes in v8:
time: 133 us
  Pallas kernels  131 us (98%)
  local copies, waits for them, and re-layouts  1.75 us (1%)
    pallas_call x1, Pallas kernels, give(): pl.pallas_call(give_kernel, out_shape=jax.ShapeDtypeStruct((3, 128, 4096)...  61.9 us
    pallas_call x1, Pallas kernels, fetch(): pl.pallas_call(fetch_kernel, out_shape=(jax.ShapeDtypeStruct((32, 2, 512,...  53.3 us
    pallas_call x1, Pallas kernels, attend(): pl.pallas_call(attend_kernel, out_shape=(jax.ShapeDtypeStruct((64, BS, DH...  15.5 us

profile of v8, /device:TPU:33, one launch (start us, length us, event | category | flops | bytes accessed | tf_op | source)
XLA Modules:
  0.0 133.0 jit_solution(4086162826477809928)
XLA Ops:
  0.6 53.3 %shard_map.94 = (bf16[32,2,512,128]{3,2,1,0:T(8,128)(2,1)S(1)}, bf16[8,2,512,128]{3,2,1,0:T(8,128)(2,1)S(1)}, f32[8,8,128]{2,1,0:T(8,128)S(1)}, f32[512,64,128]{2,1,0:T(8,128)S(1)}) custom-call(bf16[512,1024]{1,0:T(8,128)(2,1)} %k_ref.1, bf16[512,1024]{1,0:T(8,128)(2,1)} %v_ref.1, bf16[512,1024]{1,0:T(8,128)(2,1)} %q_ref.1, bf16[512,1024]{1,0:T(8,128)(2,1)} %g_ref.1, ...), custom_call_target="tpu_custom_call" | custom-call | tf_op jit(solution)/shard_map/pallas_call | solution.py:248
  53.9 15.5 %shard_map.95 = (bf16[64,64,128]{2,1,0:T(8,128)(2,1)S(1)}, f32[512,64,128]{2,1,0:T(8,128)S(1)}) custom-call(s32[3,8,256]{2,1,0:T(8,128)} %bitcast.15, s32[2]{0:T(128)} %glob.1, bf16[128,64,128]{2,1,0:T(8,128)(2,1)S(1)} %bitcast.13, f32[8,8,128]{2,1,0:T(8,128)S(1)} %get-tuple-element.10.rd_ref, ...), custom_call_target="tpu_custom_call", output_to_operand_aliasing={{1}: (5, {})} | custom-call | tf_op jit(solution)/shard_map/pallas_call | solution.py:515
  69.4 61.9 %shard_map.96 = bf16[3,128,4096]{2,1,0:T(8,128)(2,1)S(1)} custom-call(bf16[8,512,128]{2,1,0:T(8,128)(2,1)S(1)} %bitcast.14, f32[32,2,512,128]{3,2,1,0:T(8,128)S(1)} %bitcast.11), custom_call_target="tpu_custom_call" | custom-call | tf_op jit(solution)/shard_map/pallas_call | solution.py:398
  131.2 1.8 %slice_bitcast_fusion = (bf16[128,4096]{1,0:T(8,128)(2,1)}, bf16[128,4096]{1,0:T(8,128)(2,1)}, bf16[128,4096]{1,0:T(8,128)(2,1)}) fusion(bf16[3,128,4096]{2,1,0:T(8,128)(2,1)S(1)} %shard_map.96), kind=kLoop, calls=%fused_computation | loop fusion | bytes 6291456 | tf_op jit(solution)/shard_map/squeeze | solution.py:549
